TPU v7x, 32 devices: a whole 2x2x4 slice. The times are simulated.
32 devices in a mesh: seq: 16 (over z, y, x), tp: 2 (over core).
Axes of the slice: x: 2, y: 2, z: 4, core: 2. Of those that a mesh axis runs over, the one named last changes fastest.
Arguments:
- latent: bfloat16 [4096, 4096], P('seq', 'tp'), may hold values from -4000 to 4000
- latent_gain: bfloat16 [4096], P('tp'), may hold values from 0.099609375 to 1.8984375
- proj_weight: bfloat16 [4096, 1024], P('tp'), may hold values from -0.09375 to 0.09375
- patch_starts: int32 [4096], replicated, may hold values from 0 to 16383, as said below
- stream: bfloat16 [16384, 1024], P('seq'), may hold values from -500 to 500
- doc_starts: int32 [16384], P('seq'), may hold values from 0 to 16383, as said below
- stream_gain: bfloat16 [1024], replicated, may hold values from 0.099609375 to 1.8984375
- self_query: bfloat16 [1024, 1024], P(None, 'tp'), may hold values from -2 to 2
- self_key: bfloat16 [1024, 1024], P(None, 'tp'), may hold values from -2 to 2
- self_value: bfloat16 [1024, 1024], P(None, 'tp'), may hold values from -0.1875 to 0.1875
- self_out: bfloat16 [1024, 1024], P('tp'), may hold values from -0.1875 to 0.1875
- cross_query: bfloat16 [1024, 1024], P(None, 'tp'), may hold values from -2 to 2
- cross_key: bfloat16 [1024, 1024], P(None, 'tp'), may hold values from -2 to 2
- cross_value: bfloat16 [1024, 1024], P(None, 'tp'), may hold values from -0.1875 to 0.1875
- cross_out: bfloat16 [1024, 1024], P('tp'), may hold values from -0.1875 to 0.1875
Outputs:
- update: bfloat16 [16384, 1024], P('seq', 'tp')
Inputs may be any that keep to these rules, and one draw needn't show every extreme that they name: Strictly rising with patch_starts[0] = 0. In aligned blocks of 512 bytes, the patches that start in block b are numbers c(b) to c(b + 1) - 1 with c(b) within 32 of b * 128, and a patch starts at byte b * 512 + 512 // 2 of every block. The patches that start in bytes d * 1024 - 512 to (d + 1) * 1024 - 1 number at most 448 for every d, and exactly 448 for some d. doc_starts[i] is the first byte of byte i's document: never falling, at most i, always a patch start, and equal to i exactly where a document begins.
All inputs are finite; a program needn't handle non-finite values.
Results may differ from a plain program's by a relative error of at most 0.015.
The roundings to bfloat16 on the way count: a program that leaves them out, or rounds other values in their place, can miss the bound.
Values may be sent and summed in bfloat16 or wider, within the bound.
A program may use at most 128 MiB of HBM per device.

v0:
```python
import jax
import jax.numpy as jnp
from jax import lax
from jax.sharding import PartitionSpec as P

HD = 64
WIN = 512
PMAX = 448


def from_behind(array, axis, by):
    devices = lax.axis_size(axis)
    pairs = [(i, i + by) for i in range(devices) if 0 <= i + by < devices]
    return lax.ppermute(array, axis, pairs)


def norm_rows(values, gain):
    widened = values.astype(jnp.float32)
    mean_square = jnp.mean(widened * widened, axis=1, keepdims=True)
    return (widened * lax.rsqrt(mean_square + 1e-05) * gain.astype(jnp.float32)).astype(
        jnp.bfloat16
    )


def project(left, right):
    return jnp.dot(left, right, preferred_element_type=jnp.float32).astype(jnp.bfloat16)


def attend(query, all_keys, all_values, allowed, head_size):
    row_count = query.shape[0]
    key_count = all_keys.shape[0]
    head_count = query.shape[1] // head_size
    query_heads = query.reshape(row_count, head_count, head_size)
    key_heads = all_keys.reshape(key_count, head_count, head_size)
    value_heads = all_values.reshape(key_count, head_count, head_size)
    scores = jnp.einsum(
        "rhd,khd->hrk", query_heads, key_heads, preferred_element_type=jnp.float32
    ) * head_size ** (-0.5)
    scores = jnp.where(allowed[None], scores, -1e30)
    row_max = jnp.max(scores, axis=2, keepdims=True)
    weights = jnp.where(allowed[None], jnp.exp(scores - row_max), 0.0)
    row_total = jnp.sum(weights, axis=2, keepdims=True)
    probs = (weights / row_total).astype(jnp.bfloat16)
    head_mix = jnp.einsum("hrk,khd->rhd", probs, value_heads, preferred_element_type=jnp.float32)
    return head_mix.reshape(row_count, head_count * head_size).astype(jnp.bfloat16)


def on_device(
    latent,
    latent_gain,
    proj_weight,
    patch_starts,
    stream,
    doc_starts,
    stream_gain,
    self_query,
    self_key,
    self_value,
    self_out,
    cross_query,
    cross_key,
    cross_value,
    cross_out,
):
    seg_bytes = stream.shape[0]
    patch_dev = latent.shape[0]
    slot_count = PMAX
    seq_place = lax.axis_index("seq")
    first_byte = seq_place * seg_bytes
    total_bytes = seg_bytes * lax.axis_size("seq")
    head_size = HD
    widened = latent.astype(jnp.float32)
    square_sum = lax.psum(jnp.sum(widened * widened, axis=1), "tp")
    full_width = latent.shape[1] * lax.axis_size("tp")
    latent_normed = (
        widened
        * lax.rsqrt(square_sum / full_width + 1e-05)[:, None]
        * latent_gain.astype(jnp.float32)
    ).astype(jnp.bfloat16)
    partial_value = jnp.dot(latent_normed, proj_weight, preferred_element_type=jnp.float32)
    offset = jnp.sum((patch_starts < first_byte - WIN).astype(jnp.int32))
    anchor = offset - (seq_place - 1) * patch_dev
    rep_share = lax.psum_scatter(partial_value, "tp", scatter_dimension=1, tiled=True).astype(
        jnp.bfloat16
    )
    arrived = [from_behind(rep_share, "seq", towards) for towards in (1, -1)]
    joined = jnp.concatenate([arrived[0], rep_share, arrived[1]], axis=0)
    own_rows = lax.dynamic_slice_in_dim(joined, anchor, slot_count, 0)
    block_piece = lax.all_gather(own_rows, "tp", axis=1, tiled=True)
    key_total = jnp.dot(block_piece, cross_key, preferred_element_type=jnp.float32)
    value_total = jnp.dot(block_piece, cross_value, preferred_element_type=jnp.float32)
    patch_keys = key_total.astype(jnp.bfloat16)
    patch_values = value_total.astype(jnp.bfloat16)
    hidden = norm_rows(stream, stream_gain)
    own_query = project(hidden, self_query)
    own_key = project(hidden, self_key)
    own_value = project(hidden, self_value)
    cross_rows = project(hidden, cross_query)
    tail_rows = jnp.stack([own_key[seg_bytes - WIN :], own_value[seg_bytes - WIN :]])
    halo_rows = from_behind(tail_rows, "seq", 1)
    near_keys = jnp.concatenate([halo_rows[0], own_key], axis=0)
    near_values = jnp.concatenate([halo_rows[1], own_value], axis=0)
    positions = first_byte + jnp.arange(seg_bytes, dtype=jnp.int32)
    key_pos = first_byte - WIN + jnp.arange(WIN + seg_bytes, dtype=jnp.int32)
    allowed = (
        (key_pos[None, :] <= positions[:, None])
        & (key_pos[None, :] >= positions[:, None] - WIN)
        & (key_pos[None, :] >= doc_starts[:, None])
    )
    self_mixed = attend(own_query, near_keys, near_values, allowed, head_size)
    patch_total = patch_starts.shape[0]
    slot_index = offset + jnp.arange(slot_count, dtype=jnp.int32)
    slot_starts = jnp.where(
        slot_index < patch_total,
        jnp.take(patch_starts, jnp.minimum(slot_index, patch_total - 1)),
        total_bytes,
    )
    cross_allowed = (
        (slot_starts[None, :] <= positions[:, None])
        & (slot_starts[None, :] >= doc_starts[:, None])
        & (slot_starts[None, :] >= positions[:, None] - WIN)
    )
    cross_mixed = attend(cross_rows, patch_keys, patch_values, cross_allowed, head_size)
    partial_out = jnp.dot(self_mixed, self_out, preferred_element_type=jnp.float32) + jnp.dot(
        cross_mixed, cross_out, preferred_element_type=jnp.float32
    )
    return lax.psum_scatter(partial_out.astype(jnp.bfloat16), "tp", scatter_dimension=1, tiled=True)


def solution(mesh):
    in_specs = (
        P("seq", "tp"),
        P("tp"),
        P("tp", None),
        P(),
        P("seq", None),
        P("seq"),
        P(),
        P(None, "tp"),
        P(None, "tp"),
        P(None, "tp"),
        P("tp", None),
        P(None, "tp"),
        P(None, "tp"),
        P(None, "tp"),
        P("tp", None),
    )
    out_specs = P("seq", "tp")
    return jax.shard_map(
        on_device, mesh=mesh, in_specs=in_specs, out_specs=out_specs, check_vma=False
    )
```

profile of v0, /device:TPU:0, one launch (start us, length us, event | category | flops | bytes accessed | tf_op | source)
XLA Modules:
  0.0 159.6 jit_solution(10256125406882558382)
XLA Ops:
  6.5 0.0 copy-start
  6.5 0.0 copy-start.3
  6.5 0.0 reduce-scatter.3.cloned.1.call-start
  6.5 2.2 %fusion.14 = f32[1024]{0:T(1024)S(1)} fusion(bf16[1024,1024]{1,0:T(8,128)(2,1)} %param.19), kind=kLoop, calls=%fused_computation.23 | loop fusion | flops 3144704 | bytes 2101248 | tf_op jit(solution)/shard_map/reduce_sum | solution.py:19
  8.8 0.7 convert_element_type.70
  9.5 3.3 %convolution_convert_fusion.2 = bf16[1024,512]{0,1:T(8,128)(2,1)S(1)} fusion(bf16[1024,512]{1,0:T(8,128)(2,1)} %param.24, bf16[1024,1024]{1,0:T(8,128)(2,1)} %param.19, f32[1024]{0:T(1024)S(1)} %convert_element_type.70, f32[1024]{0:T(1024)S(1)} %add_rsqrt_fusion), kind=kOutput, calls=%fused_computation.41 | convolution fusion | flops 1078460416 | bytes 4202496 | tf_op jit(solution)/shard_map/dot_general | solution.py:26
  12.7 0.0 copy-done.3
  12.7 0.0 copy-done.11
  12.8 0.0 copy-start.7
  12.8 0.0 copy-start.10
  12.8 0.0 copy-start.4
  12.8 1.4 convolution_convert_fusion.3
  14.2 0.0 copy-start.8
  14.2 0.1 slice_bitcast_fusion
  14.3 0.0 copy-done.7
  14.4 1.2 pad_maximum_fusion.1
  15.6 0.0 copy-done.8
  15.6 5.9 %collective-permute-start = (bf16[2,512,512]{1,2,0:T(8,128)(2,1)}, bf16[2,512,512]{1,2,0:T(8,128)(2,1)}, u32[]{:S(2)}, u32[]{:S(2)}) collective-permute-start(bf16[2,512,512]{1,2,0:T(8,128)(2,1)} %pad_maximum_fusion.1), channel_id=1, source_target_pairs={{0,2},{2,4},{4,6},{6,8},{8,10},{10,12},{12,14},{14,16},{16,18},{18... | collective-permute-start | bytes 3145736 | tf_op jit(solution)/shard_map/ppermute | solution.py:14
  21.5 0.0 copy-done.10
  21.5 0.0 copy-done.4
  21.5 0.3 fusion.19
  21.7 2.5 %psum.7 = f32[256]{0:T(256)S(1)} all-reduce(f32[256]{0:T(256)S(1)} %fusion.19), channel_id=1, replica_groups=mesh['seq'=16,'tp'=2] {'tp'}, use_global_device_ids=true, to_apply=%region_4.0 | all-reduce | flops 256 | bytes 2048 | tf_op jit(solution)/shard_map/psum | solution.py:73
  24.2 4.8 %fusion.29 = f32[256,1024]{1,0:T(8,128)} fusion(bf16[2048,1024]{1,0:T(8,128)(2,1)} %param.17, bf16[256,2048]{1,0:T(8,128)(2,1)} %param.15, f32[2048]{0:T(1024)S(1)} %convert_element_type.80, f32[256]{0:T(256)S(1)} %add_rsqrt_fusion.1), kind=kOutput, calls=%fused_computation.46 | convolution fusion | flops 1075838976 | bytes 6300672 | tf_op jit(solution)/shard_map/dot_general | solution.py:80
  29.0 0.0 reduce-scatter.3.cloned.1.call-update
  29.1 0.0 reduce-scatter.5.cloned.1.call-start
  29.1 0.0 copy-start.9
  29.1 3.6 %convolution_convert_fusion.1 = bf16[1024,512]{0,1:T(8,128)(2,1)} fusion(bf16[1024,512]{1,0:T(8,128)(2,1)} %param.22, bf16[1024,1024]{1,0:T(8,128)(2,1)S(1)} %copy-done.3, f32[1024]{0:T(1024)S(1)} %convert_element_type.70, f32[1024]{0:T(1024)S(1)} %add_rsqrt_fusion), kind=kOutput, calls=%fused_computation.40 | convolution fusion | flops 1078460416 | bytes 4202496 | tf_op jit(solution)/shard_map/dot_general | solution.py:26
  32.8 0.0 copy-done.1
  32.8 0.6 convert_reduce_fusion
  33.4 0.6 compare_select_fusion
  34.0 3.0 %gather_fusion = s32[448]{0:T(512)S(1)} fusion(s32[4096]{0:T(1024)S(1)} %copy-done.1, s32[1024]{0:T(1024)S(1)} %pad_clamp_fusion), kind=kCustom, calls=%fused_computation | custom fusion | bytes 5376 | tf_op jit(solution)/shard_map/jit(_take)/gather | solution.py:115
  37.0 0.6 select_select_fusion
  37.6 0.0 copy-done.9
  37.6 1.3 compare_and_fusion.1
  39.5 3.6 %convolution_convert_fusion = bf16[1024,512]{0,1:T(8,128)(2,1)} fusion(bf16[1024,512]{1,0:T(8,128)(2,1)} %param.26, bf16[1024,1024]{1,0:T(8,128)(2,1)S(1)} %copy-done.3, f32[1024]{0:T(1024)S(1)} %convert_element_type.70, f32[1024]{0:T(1024)S(1)} %add_rsqrt_fusion), kind=kOutput, calls=%fused_computation.39 | convolution fusion | flops 1078460416 | bytes 4202496 | tf_op jit(solution)/shard_map/dot_general | solution.py:26
  43.2 2.1 %compare_and_fusion = pred[1024,1536]{1,0:T(8,128)(4,1)S(1)} fusion(s32[1536]{0:T(1024)S(1)} %iota_add_fusion, s32[1024]{0:T(1024)S(1)} %copy-done.9, s32[1024]{0:T(1024)S(1)} %get-tuple-element.12, s32[1024]{0:T(1024)S(1)} %get-tuple-element.11), kind=kLoop, calls=%fused_computation.19 | loop fusion | flops 7864320 | bytes 1591296 | tf_op jit(solution)/shard_map/and | solution.py:106
  45.3 0.0 collective-permute-done
  45.3 2.1 %fusion.50 = (bf16[1,512,512]{1,2,0:T(8,128)(2,1)S(1)}, bf16[1,512,512]{1,2,0:T(8,128)(2,1)}) fusion(bf16[2,512,512]{1,2,0:T(8,128)(2,1)} %collective-permute-done), kind=kLoop, calls=%fused_computation.77 | loop fusion | bytes 2097152 | tf_op jit(solution)/shard_map/slice | solution.py:102
  47.4 29.0 %fusion.51 = (f32[8,1024]{1,0:T(8,128)S(1)}, f32[8,1024,1536]{2,1,0:T(8,128)}) fusion(pred[1024,1536]{1,0:T(8,128)(4,1)S(1)} %compare_and_fusion, bf16[1024,8,64]{0,2,1:T(8,128)(2,1)} %bitcast.49, bf16[1024,8,64]{0,2,1:T(8,128)(2,1)} %bitcast.46, bf16[512,8,64]{0,2,1:T(8,128)(2,1)} %bitcast.44), kind=kOutput, calls=%fused_computation.78 | convolution fusion | flops 1676674560 | bytes 54558720 | tf_op jit(solution)/shard_map/sub | solution.py:41
  76.4 18.0 %fusion.26 = bf16[8,64,1024]{2,1,0:T(8,128)(2,1)S(1)} fusion(f32[8,1024,1536]{2,1,0:T(8,128)} %get-tuple-element.8, f32[8,1024]{1,0:T(8,128)S(1)} %get-tuple-element.7, bf16[1024,8,64]{0,2,1:T(8,128)(2,1)} %bitcast.45, bf16[512,8,64]{0,2,1:T(8,128)(2,1)S(1)} %bitcast.43), kind=kOutput, calls=%fused_computation.43 | convolution fusion | flops 1639448576 | bytes 52985856 | tf_op jit(solution)/shard_map/hrk,khd->rhd/dot_general | solution.py:44
  94.4 0.0 reduce-scatter.3.cloned.1.call-done
  94.5 1.1 convert_element_type.82
  95.5 2.4 %collective-permute-start.1 = (bf16[256,512]{1,0:T(8,128)(2,1)S(1)}, bf16[256,512]{1,0:T(8,128)(2,1)S(1)}, u32[]{:S(2)}, u32[]{:S(2)}) collective-permute-start(bf16[256,512]{1,0:T(8,128)(2,1)S(1)} %convert_element_type.82), channel_id=1, source_target_pairs={{0,2},{2,4},{4,6},{6,8},{8,10},{10,12},{12,14},{14,16},{16,18},{18... | collective-permute-start | bytes 786440 | tf_op jit(solution)/shard_map/ppermute | solution.py:14
  98.0 1.5 collective-permute-start.2
  99.5 0.0 copy-done
  99.5 0.0 copy-start.12
  99.5 3.3 %fusion.53 = f32[1024,1024]{1,0:T(8,128)} fusion(bf16[1024,512]{0,1:T(8,128)(2,1)S(1)} %bitcast.39, bf16[512,1024]{1,0:T(8,128)(2,1)S(1)} %copy-done), kind=kOutput, calls=%fused_computation.80 | convolution fusion | flops 1073741824 | bytes 6291456 | tf_op jit(solution)/shard_map/dot_general | solution.py:124
  102.8 1.1 collective-permute-done.1
  103.9 7.5 %collective-permute-done.2 = bf16[256,512]{1,0:T(8,128)(2,1)S(1)} collective-permute-done((bf16[256,512]{1,0:T(8,128)(2,1)S(1)}, bf16[256,512]{1,0:T(8,128)(2,1)S(1)}, u32[]{:S(2)}, u32[]{:S(2)}) %collective-permute-start.2) | collective-permute-done | bytes 262176 | tf_op jit(solution)/shard_map/ppermute | solution.py:14
  111.4 1.1 fusion.35
  112.5 2.5 %all_gather.3 = bf16[448,1024]{1,0:T(8,128)(2,1)S(1)} all-gather(bf16[448,512]{1,0:T(8,128)(2,1)S(1)} %fusion.35), channel_id=1, replica_groups=mesh['seq'=16,'tp'=2] {'tp'}, dimensions={1}, use_global_device_ids=true | all-gather | bytes 1376256 | tf_op jit(solution)/shard_map/all_gather | solution.py:89
  115.0 0.0 copy-done.12
  115.0 1.4 convolution_convert_fusion.4
  116.4 1.2 copy.19
  117.6 2.7 %convolution_convert_fusion.5 = bf16[448,512]{1,0:T(8,128)(2,1)} fusion(bf16[448,1024]{1,0:T(8,128)(2,1)S(1)} %all_gather.3, bf16[1024,512]{1,0:T(8,128)(2,1)} %param.28), kind=kOutput, calls=%fused_computation.45 | convolution fusion | flops 469991424 | bytes 2424832 | tf_op jit(solution)/shard_map/dot_general | solution.py:91
  120.3 2.0 %copy.18 = bf16[448,512]{0,1:T(8,128)(2,1)} copy(bf16[448,512]{1,0:T(8,128)(2,1)} %convolution_convert_fusion.5) | data formatting | bytes 917504 | tf_op jit(solution)/shard_map/convert_element_type | solution.py:93
  122.3 0.0 copy-done.6
  122.3 10.4 %fusion.52 = (f32[8,1024]{1,0:T(8,128)S(1)}, f32[8,1024,448]{1,2,0:T(8,128)}) fusion(pred[1024,448]{0,1:T(8,128)(4,1)S(1)} %copy-done.6, bf16[1024,8,64]{0,2,1:T(8,128)(2,1)} %bitcast.48, bf16[448,8,64]{0,2,1:T(8,128)(2,1)S(1)} %bitcast.41), kind=kOutput, calls=%fused_computation.79 | convolution fusion | flops 488112576 | bytes 16678912 | tf_op jit(solution)/shard_map/sub | solution.py:41
  132.7 6.9 %fusion.25 = bf16[8,64,1024]{2,1,0:T(8,128)(2,1)S(1)} fusion(bf16[448,8,64]{0,2,1:T(8,128)(2,1)} %bitcast.42, f32[8,1024,448]{1,2,0:T(8,128)} %get-tuple-element.10, f32[8,1024]{1,0:T(8,128)S(1)} %get-tuple-element.9), kind=kOutput, calls=%fused_computation.38 | convolution fusion | flops 477626368 | bytes 16220160 | tf_op jit(solution)/shard_map/hrk,khd->rhd/dot_general | solution.py:44
  139.5 0.0 copy-done.2
  139.6 0.0 copy-done.5
  139.6 2.8 %add_convert_fusion = bf16[1024,1024]{1,0:T(8,128)(2,1)} fusion(f32[1024,1024]{1,0:T(8,128)S(1)} %copy-done.2, bf16[1024,512]{0,1:T(8,128)(2,1)S(1)} %bitcast.40, bf16[512,1024]{1,0:T(8,128)(2,1)S(1)} %copy-done.5), kind=kOutput, calls=%fused_computation.26 | convolution fusion | flops 1075838976 | bytes 8388608 | tf_op jit(solution)/shard_map/dot_general | solution.py:124
  142.3 0.0 reduce-scatter.5.cloned.1.call-update
  142.3 10.4 %reduce-scatter.5.cloned.1.call-done = bf16[1024,512]{1,0:T(8,128)(2,1)} async-done(((bf16[1024,1024]{1,0:T(8,128)(2,1)}), bf16[1024,512]{1,0:T(8,128)(2,1)}) %reduce-scatter.5.cloned.1.call-update) | async-done | bytes 1048592 | tf_op jit(solution)/shard_map/reduce_scatter | solution.py:127
  (11 shorter events, 0.0 us)
Async XLA Ops:
  6.5 93.0 %copy-start = (bf16[512,1024]{1,0:T(8,128)(2,1)S(1)}, bf16[512,1024]{1,0:T(8,128)(2,1)}, u32[]{:S(2)}) copy-start(bf16[512,1024]{1,0:T(8,128)(2,1)} %param.25) | copy-start | bytes 3145732
  6.5 6.2 %copy-start.3 = (bf16[1024,1024]{1,0:T(8,128)(2,1)S(1)}, bf16[1024,1024]{1,0:T(8,128)(2,1)}, u32[]{:S(2)}) copy-start(bf16[1024,1024]{1,0:T(8,128)(2,1)} %param.19) | copy-start | bytes 6291460
  6.5 87.9 %reduce-scatter.3.cloned.1.call-start = ((), (), s32[]{:S(2)}) async-start(), calls=%async_computation.2 | async-start | bytes 1572864 | tf_op jit(solution)/shard_map/reduce_scatter | solution.py:83
  6.5 6.2 %copy-start.11 = (bf16[1024,512]{1,0:T(8,128)(2,1)S(1)}, bf16[1024,512]{1,0:T(8,128)(2,1)}, u32[]{:S(2)}) copy-start(bf16[1024,512]{1,0:T(8,128)(2,1)} %param.23) | copy-start | bytes 3145732
  12.8 1.6 copy-start.7
  12.8 8.7 %copy-start.10 = (bf16[2048]{0:T(1024)(128)(2,1)S(1)}, bf16[2048]{0:T(1024)(128)(2,1)}, u32[]{:S(2)}) copy-start(bf16[2048]{0:T(1024)(128)(2,1)} %param.16) | copy-start | bytes 12292
  12.8 8.7 %copy-start.4 = (bf16[256,2048]{1,0:T(8,128)(2,1)S(1)}, bf16[256,2048]{1,0:T(8,128)(2,1)}, u32[]{:S(2)}) copy-start(bf16[256,2048]{1,0:T(8,128)(2,1)} %param.15) | copy-start | bytes 3145732
  14.2 1.4 copy-start.8
  15.6 29.7 %collective-permute-start = (bf16[2,512,512]{1,2,0:T(8,128)(2,1)}, bf16[2,512,512]{1,2,0:T(8,128)(2,1)}, u32[]{:S(2)}, u32[]{:S(2)}) collective-permute-start(bf16[2,512,512]{1,2,0:T(8,128)(2,1)} %pad_maximum_fusion.1), channel_id=1, source_target_pairs={{0,2},{2,4},{4,6},{6,8},{8,10},{10,12},{12,14},{14,16},{16,18},{18... | collective-permute-start | bytes 3145736 | tf_op jit(solution)/shard_map/ppermute | solution.py:14
  29.0 3.7 %copy-start.1 = (s32[4096]{0:T(1024)S(1)}, s32[4096]{0:T(1024)}, u32[]{:S(2)}) copy-start(s32[4096]{0:T(1024)} %param.18) | copy-start | bytes 49156
  29.1 123.7 %reduce-scatter.5.cloned.1.call-start = ((), (), s32[]{:S(2)}) async-start(), calls=%async_computation.3 | async-start | bytes 3145728 | tf_op jit(solution)/shard_map/reduce_scatter | solution.py:127
  29.1 8.5 %copy-start.9 = (s32[1024]{0:T(1024)S(1)}, s32[1024]{0:T(1024)}, u32[]{:S(2)}) copy-start(s32[1024]{0:T(1024)} %param.20) | copy-start | bytes 12292
  95.5 8.4 %collective-permute-start.1 = (bf16[256,512]{1,0:T(8,128)(2,1)S(1)}, bf16[256,512]{1,0:T(8,128)(2,1)S(1)}, u32[]{:S(2)}, u32[]{:S(2)}) collective-permute-start(bf16[256,512]{1,0:T(8,128)(2,1)S(1)} %convert_element_type.82), channel_id=1, source_target_pairs={{0,2},{2,4},{4,6},{6,8},{8,10},{10,12},{12,14},{14,16},{16,18},{18... | collective-permute-start | bytes 786440 | tf_op jit(solution)/shard_map/ppermute | solution.py:14
  98.0 13.4 %collective-permute-start.2 = (bf16[256,512]{1,0:T(8,128)(2,1)S(1)}, bf16[256,512]{1,0:T(8,128)(2,1)S(1)}, u32[]{:S(2)}, u32[]{:S(2)}) collective-permute-start(bf16[256,512]{1,0:T(8,128)(2,1)S(1)} %convert_element_type.82), channel_id=1, source_target_pairs={{2,0},{4,2},{6,4},{8,6},{10,8},{12,10},{14,12},{16,14},{18,16},{20... | collective-permute-start | bytes 786440 | tf_op jit(solution)/shard_map/ppermute | solution.py:14
  99.5 15.4 %copy-start.12 = (bf16[1024,512]{1,0:T(8,128)(2,1)S(1)}, bf16[1024,512]{1,0:T(8,128)(2,1)}, u32[]{:S(2)}) copy-start(bf16[1024,512]{1,0:T(8,128)(2,1)} %param.27) | copy-start | bytes 3145732
  115.0 7.3 %copy-start.6 = (pred[1024,448]{0,1:T(8,128)(4,1)S(1)}, pred[1024,448]{0,1:T(8,128)(4,1)}, u32[]{:S(2)}) copy-start(pred[1024,448]{0,1:T(8,128)(4,1)} %compare_and_fusion.1) | copy-start | bytes 1376260
  132.7 6.9 %copy-start.2 = (f32[1024,1024]{1,0:T(8,128)S(1)}, f32[1024,1024]{1,0:T(8,128)}, u32[]{:S(2)}) copy-start(f32[1024,1024]{1,0:T(8,128)} %fusion.53) | copy-start | bytes 12582916
  132.7 6.9 %copy-start.5 = (bf16[512,1024]{1,0:T(8,128)(2,1)S(1)}, bf16[512,1024]{1,0:T(8,128)(2,1)}, u32[]{:S(2)}) copy-start(bf16[512,1024]{1,0:T(8,128)(2,1)} %param.29) | copy-start | bytes 3145732
Sparse Core Ops, SparseCore 0:
  29.2 7.7 reduce-scatter.2
  142.5 10.2 reduce-scatter.4
where the time goes:
time: 160 us
  matrix products  91.1 us (57%)
  waiting for transfers between devices  19.1 us (12%)
  between operations  14.3 us (9%)
  other arithmetic  11.8 us (7%)
  starting transfers between devices  9.86 us (6%)
  local copies, waits for them, and re-layouts  8.5 us (5%)
  blocking collectives  4.93 us (3%)
    sub x2, matrix products, attend(): weights = jnp.where(allowed[None], jnp.exp(scores - row_max), 0.0)  39.4 us
    dot_general x2, matrix products, attend(): jnp.einsum('hrk,khd->rhd', probs, value_heads, preferred_element_type=jnp...  24.9 us
    dot_general x4, matrix products, project(): jnp.dot(left, right, preferred_element_type=jnp.float32)  11.9 us
    reduce_scatter x1, waiting for transfers between devices, on_device(): lax.psum_scatter(partial_out.astype(jnp.bfloat16), 'tp', scatter_dimensio...  10.4 us
    ppermute x3, starting transfers between devices, from_behind(): return lax.ppermute(array, axis, pairs)  9.82 us
    ppermute x3, waiting for transfers between devices, from_behind(): return lax.ppermute(array, axis, pairs)  8.62 us
    dot_general x1, matrix products, on_device(): jnp.dot(latent_normed, proj_weight, preferred_element_type=jnp.float32)  4.8 us
    dot_general x1, matrix products, on_device(): jnp.dot(self_mixed, self_out, preferred_element_type=jnp.float32)  3.27 us
  transfers between devices with their start and end apart: 5, of which 3 were waited for; matrix products, arithmetic and copies ran while one was open for 46% of the time, Pallas kernels for 0%

commit v1 on v0

v1 whole, which is shorter than its diff:
```python
import functools

import jax
import jax.numpy as jnp
from jax import lax
from jax.experimental import pallas as pl
from jax.experimental.pallas import tpu as pltpu
from jax.sharding import PartitionSpec as P

HD = 64
WIN = 512
DRIFT = 32
LANES = 128
QB = 256
F32 = jnp.float32
BF16 = jnp.bfloat16
FAR = -1e30


def shift(array, axis, by):
    devices = lax.axis_size(axis)
    pairs = [(i, i + by) for i in range(devices) if 0 <= i + by < devices]
    return lax.ppermute(array, axis, pairs)


def swap(array):
    return lax.ppermute(array, "tp", [(0, 1), (1, 0)])


def norm_rows(values, gain):
    widened = values.astype(F32)
    mean_square = jnp.mean(widened * widened, axis=1, keepdims=True)
    return (widened * lax.rsqrt(mean_square + 1e-05) * gain.astype(F32)).astype(BF16)


def mm(left, right):
    return jnp.dot(left, right, preferred_element_type=F32)


def pair_attend(query, keys, values, bias):
    rows = query.shape[0]
    low = lax.broadcasted_iota(jnp.int32, (rows, LANES), 1) < HD
    zero = jnp.zeros_like(query)
    scaled = query * jnp.asarray(HD**-0.5, BF16)
    both = jnp.concatenate([jnp.where(low, scaled, zero), jnp.where(low, zero, scaled)], axis=0)
    scores = lax.dot_general(both, keys, (((1,), (1,)), ((), ())), preferred_element_type=F32)
    wide = jnp.concatenate([values, jnp.ones_like(values)], axis=1)
    mixed = []
    for half in range(2):
        one = scores[half * rows : (half + 1) * rows] + bias
        top = jnp.max(one, axis=1, keepdims=True)
        weights = jnp.exp(one - top).astype(BF16)
        total = mm(weights, wide)
        mixed.append(total[:, :LANES] / total[:, LANES:])
    return jnp.where(low, mixed[0], mixed[1]).astype(BF16)


def proj_kernel(stream, gain, wk, wv, wq, wc, k_out, v_out, q_out, c_out):
    hidden = norm_rows(stream[...], gain[...])
    for weight, out in ((wk, k_out), (wv, v_out), (wq, q_out), (wc, c_out)):
        out[...] = mm(hidden, weight[...]).astype(BF16)


def self_kernel(q, k, v, mine, other, gain, wk, wv, low_key, out, keys, values):
    step = pl.program_id(0)
    half = mine.shape[0]
    halo = 2 * half

    @pl.when(step == 0)
    def _():
        place = lax.axis_index("tp")
        for piece, at in ((mine, place), (other, 1 - place)):
            hidden = norm_rows(piece[...], gain[...])
            rows = pl.ds(pl.multiple_of(at * half, half), half)
            keys[rows, :] = mm(hidden, wk[...]).astype(BF16)
            values[rows, :] = mm(hidden, wv[...]).astype(BF16)
        keys[halo:, :] = k[...]
        values[halo:, :] = v[...]

    count = halo + QB
    base = pl.multiple_of(step * QB, QB)
    index = lax.broadcasted_iota(jnp.int32, (QB, count), 1)
    row = lax.broadcasted_iota(jnp.int32, (QB, count), 0)
    allowed = (index <= row + halo) & (index >= low_key[...] - base)
    bias = jnp.where(allowed, 0.0, FAR).astype(F32)
    for col in range(0, q.shape[1], LANES):
        cols = slice(col, col + LANES)
        out[:, cols] = pair_attend(
            q[:, cols], keys[pl.ds(base, count), cols], values[pl.ds(base, count), cols], bias
        )


def cross_kernel(
    q, rep, left_mine, left_other, right_mine, right_other, wk, wv, starts, low_key, mixed, ws, wc,
    own_out, far_out, joined, keys, values, cross,
):
    step = pl.program_id(0)
    place = lax.axis_index("tp")
    width = left_mine.shape[1]
    here = pl.ds(pl.multiple_of(place * width, width), width)
    there = pl.ds(pl.multiple_of((1 - place) * width, width), width)
    before, own, after = left_mine.shape[0], rep.shape[0], right_mine.shape[0]
    used = before + own + after

    @pl.when(step == 0)
    def _():
        joined[:before, here] = left_mine[...]
        joined[:before, there] = left_other[...]
        joined[before : before + own, :] = rep[...]
        joined[before + own :, here] = right_mine[...]
        joined[before + own :, there] = right_other[...]
        for weight, target in ((wk, keys), (wv, values)):
            target[:used, :] = mm(joined[...], weight[...]).astype(BF16)
            target[used:, :] = jnp.zeros((target.shape[0] - used, target.shape[1]), BF16)

    slots = keys.shape[0] - LANES
    per_win = WIN // QB
    base = pl.multiple_of(lax.rem(lax.div(step, per_win), 2) * LANES, LANES)
    index = starts[:, pl.ds(base, slots)]
    row = lax.broadcasted_iota(jnp.int32, (QB, slots), 0) + step * QB
    allowed = (index <= row) & (index >= low_key[...])
    bias = jnp.where(allowed, 0.0, FAR).astype(F32)
    for col in range(0, q.shape[1], LANES):
        cols = slice(col, col + LANES)
        cross[:, cols] = pair_attend(
            q[:, cols], keys[pl.ds(base, slots), cols], values[pl.ds(base, slots), cols], bias
        )
    own_out[...] = mm(mixed[...], ws[:, here]) + mm(cross[...], wc[:, here])
    far_out[...] = (mm(mixed[...], ws[:, there]) + mm(cross[...], wc[:, there])).astype(BF16)


def rows_spec(width):
    return pl.BlockSpec((QB, width), lambda i: (i, 0))


def whole(array):
    return pl.BlockSpec(array.shape, lambda i: (0,) * array.ndim)


def on_device(
    latent, latent_gain, proj_weight, patch_starts, stream, doc_starts, stream_gain,
    self_query, self_key, self_value, self_out, cross_query, cross_key, cross_value, cross_out,
):
    seg, width = stream.shape
    patch_dev = latent.shape[0]
    cols = self_query.shape[1]
    place = lax.axis_index("tp")
    seq_place = lax.axis_index("seq")
    steps = seg // QB
    gain = stream_gain[None, :]
    params = pltpu.CompilerParams(dimension_semantics=("arbitrary",), vmem_limit_bytes=48 << 20)

    half = WIN // 2
    tail = lax.dynamic_slice_in_dim(stream, seg - WIN + place * half, half, 0)
    halo_mine = shift(tail, "seq", 1)
    halo_other = swap(halo_mine)

    widened = latent.astype(F32)
    square = jnp.sum(widened * widened, axis=1)
    square_sum = square + swap(square)

    piece = jax.ShapeDtypeStruct((seg, cols), BF16)
    own_key, own_value, own_query, cross_rows = pl.pallas_call(
        proj_kernel,
        grid=(steps,),
        in_specs=[rows_spec(width), whole(gain)] + [whole(self_key)] * 4,
        out_specs=[rows_spec(cols)] * 4,
        out_shape=[piece] * 4,
        compiler_params=params,
        cost_estimate=pl.CostEstimate(flops=8 * seg * width * cols, bytes_accessed=12 << 20, transcendentals=0),
    )(stream, gain, self_key, self_value, self_query, cross_query)

    full_width = latent.shape[1] * lax.axis_size("tp")
    latent_normed = (
        widened * lax.rsqrt(square_sum / full_width + 1e-05)[:, None] * latent_gain.astype(F32)
    ).astype(BF16)
    partial = mm(latent_normed, proj_weight)
    rep = (partial + swap(partial)).astype(BF16)
    per_win = WIN * patch_dev // seg
    before, after = per_win + DRIFT, DRIFT
    share = lax.dynamic_slice_in_dim(rep, place * cols, cols, 1)
    left_mine = shift(share[patch_dev - before :], "seq", 1)
    right_mine = shift(share[:after], "seq", -1)
    arrived = swap(jnp.concatenate([left_mine, right_mine], axis=0))
    left_other, right_other = arrived[:before], arrived[before:]

    positions = jnp.arange(seg, dtype=jnp.int32)
    low_byte = jnp.maximum(positions - WIN, doc_starts - seq_place * seg)[:, None]
    low_spec = pl.BlockSpec((QB, 1), lambda i: (i, 0))
    self_mixed = pl.pallas_call(
        self_kernel,
        grid=(steps,),
        in_specs=[
            rows_spec(cols), whole(own_key), whole(own_key), whole(tail), whole(tail),
            whole(gain), whole(self_key), whole(self_key), low_spec,
        ],
        out_specs=rows_spec(cols),
        out_shape=piece,
        scratch_shapes=[pltpu.VMEM((WIN + seg, cols), BF16)] * 2,
        compiler_params=params,
        cost_estimate=pl.CostEstimate(flops=16 << 30, bytes_accessed=6 << 20, transcendentals=seg * 8 * 768),
    )(own_query, own_key, own_value, halo_mine, halo_other, gain, self_key, self_value, low_byte + WIN)

    used = before + patch_dev + after
    slots = (used + LANES - 1) // LANES * LANES
    padded = jnp.pad(
        patch_starts - seq_place * seg, (before, slots), constant_values=seg * (lax.axis_size("seq") + 1)
    )
    window = lax.dynamic_slice_in_dim(padded, seq_place * patch_dev, slots, 0)
    window = jnp.where(jnp.arange(slots) < used, window, seg)[None, :]
    own, far = pl.pallas_call(
        cross_kernel,
        grid=(steps,),
        in_specs=[
            rows_spec(cols), whole(rep), whole(left_mine), whole(left_mine), whole(right_mine), whole(right_mine),
            whole(cross_key), whole(cross_key), whole(window), low_spec, rows_spec(cols),
            whole(self_out), whole(cross_out),
        ],
        out_specs=[rows_spec(cols)] * 2,
        out_shape=[jax.ShapeDtypeStruct((seg, cols), F32), piece],
        scratch_shapes=[
            pltpu.VMEM((used, width), BF16), pltpu.VMEM((slots, cols), BF16),
            pltpu.VMEM((slots, cols), BF16), pltpu.VMEM((QB, cols), BF16),
        ],
        compiler_params=params,
        cost_estimate=pl.CostEstimate(flops=10 << 30, bytes_accessed=8 << 20, transcendentals=seg * 8 * 384),
    )(
        cross_rows, rep, left_mine, left_other, right_mine, right_other, cross_key, cross_value,
        window, low_byte, self_mixed, self_out, cross_out,
    )
    return (own + swap(far).astype(F32)).astype(BF16)


def solution(mesh):
    in_specs = (
        P("seq", "tp"), P("tp"), P("tp", None), P(), P("seq", None), P("seq"), P(),
        P(None, "tp"), P(None, "tp"), P(None, "tp"), P("tp", None),
        P(None, "tp"), P(None, "tp"), P(None, "tp"), P("tp", None),
    )
    return jax.shard_map(
        on_device, mesh=mesh, in_specs=in_specs, out_specs=P("seq", "tp"), check_vma=False
    )
```

time: 160 us -> 77.2 us (0.48)
  matrix products: 91.1 us -> 3.89 us
  Pallas kernels: 0 us -> 35 us
  between operations: 14.3 us -> 0.26 us
  waiting for transfers between devices: 19.1 us -> 10.2 us
  other arithmetic: 11.8 us -> 6.58 us
  blocking collectives: 4.93 us -> 0 us
  starting transfers between devices: 9.86 us -> 11.8 us
    dot_general x11 -> x1, matrix products: 51.7 us -> 3.89 us  [mm(): return jnp.dot(left, right, preferred_element_type=F32)]
    sub x2 -> x0, matrix products: 39.4 us -> none  [attend(): weights = jnp.where(allowed[None], jnp.exp(scores - row_max), 0.0)]
    pallas_call x0 -> x3, Pallas kernels: none -> 35 us  [the longest x1 14.4 us: on_device(): pl.pallas_call(self_kernel, grid=(steps,), in_specs=[rows_spec(cols), who...]
    reduce_scatter x2 -> x0, waiting for transfers between devices: 10.4 us -> none  [the longest x1 10.4 us: on_device(): lax.psum_scatter(partial_out.astype(jnp.bfloat16), 'tp', scatter_dimensio...]
    unnamed x26 -> x30, local copies, waits for them, and re-layouts: 0.06 us -> 6.63 us
    and x2 -> x0, other arithmetic: 3.45 us -> none  [the longest x1 2.13 us: on_device(): (key_pos[None, :] <= positions[:, None]) & (key_pos[None, :] >= positions...]
    convert_element_type x2 -> x0, local copies, waits for them, and re-layouts: 3.24 us -> none  [the longest x1 2.02 us: on_device(): patch_values = value_total.astype(jnp.bfloat16)]
    convert_element_type x3, other arithmetic: 1.76 us -> 4.95 us  [the longest x1 2.91 us: on_device(): return (own + swap(far).astype(F32)).astype(BF16)]
  transfers between devices with their start and end apart: 5 -> 8, of which waited for: 3 -> 4; matrix products, arithmetic and copies ran while one was open for 46% -> 5% of each run, Pallas kernels for 0% -> 29%
where the time goes in v1:
time: 77.2 us; the launch traced here: 75.9 us
  Pallas kernels  35 us (45%)
  starting transfers between devices  11.8 us (15%)
  waiting for transfers between devices  10.2 us (13%)
  local copies, waits for them, and re-layouts  8.21 us (11%)
  other arithmetic  6.58 us (9%)
  matrix products  3.89 us (5%)
    pallas_call x1, Pallas kernels, on_device(): pl.pallas_call(self_kernel, grid=(steps,), in_specs=[rows_spec(cols), who...  14.4 us
    pallas_call x1, Pallas kernels, on_device(): pl.pallas_call(cross_kernel, grid=(steps,), in_specs=[rows_spec(cols), wh...  13 us
    ppermute x3, starting transfers between devices, shift(): return lax.ppermute(array, axis, pairs)  10.3 us
    ppermute x3, waiting for transfers between devices, shift(): return lax.ppermute(array, axis, pairs)  7.76 us
    pallas_call x1, Pallas kernels, on_device(): pl.pallas_call(proj_kernel, grid=(steps,), in_specs=[rows_spec(width), wh...  7.6 us
    unnamed x30, local copies, waits for them, and re-layouts  6.63 us
    dot_general x1, matrix products, mm(): return jnp.dot(left, right, preferred_element_type=F32)  3.89 us
    convert_element_type x1, other arithmetic, on_device(): return (own + swap(far).astype(F32)).astype(BF16)  2.91 us
  transfers between devices with their start and end apart: 8, of which 4 were waited for; matrix products, arithmetic and copies ran while one was open for 5% of the time, Pallas kernels for 29%

profile of v1, /device:TPU:0, one launch (start us, length us, event | category | flops | bytes accessed | tf_op | source)
XLA Modules:
  0.0 75.9 jit_solution(13663607958184829569)
XLA Ops:
  0.0 1.5 %fusion = f32[256]{0:T(256)S(1)} fusion(bf16[256,2048]{1,0:T(8,128)(2,1)} %param.15), kind=kLoop, calls=%fused_computation.2 | loop fusion | flops 1572608 | bytes 1049600 | tf_op jit(solution)/shard_map/reduce_sum | solution.py:159
  1.5 0.6 collective-permute-start
  2.1 0.7 convert_element_type.19
  2.8 0.1 collective-permute-done
  2.9 0.0 copy-start.14
  2.9 0.0 copy-start.12
  2.9 0.0 copy-start.13
  2.9 0.0 copy-start
  2.9 3.9 %fusion.3 = f32[256,1024]{1,0:T(8,128)S(1)} fusion(bf16[2048,1024]{1,0:T(8,128)(2,1)} %param.17, bf16[256,2048]{1,0:T(8,128)(2,1)} %param.15, f32[2048]{0:T(1024)S(1)} %convert_element_type.19, f32[256]{0:T(256)S(1)} %add_rsqrt_fusion), kind=kOutput, calls=%fused_computation.6 | convolution fusion | flops 1075838976 | bytes 6300672 | tf_op jit(solution)/shard_map/dot_general | solution.py:37
  6.8 0.4 collective-permute-start.1
  7.2 1.1 %constant_dynamic-slice_fusion = bf16[256,1024]{1,0:T(8,128)(2,1)S(1)} fusion(bf16[1024,1024]{1,0:T(8,128)(2,1)} %stream.1, s32[]{:T(128)S(6)} %select_n.16), kind=kLoop, calls=%fused_computation.18 | loop fusion | bytes 1048580 | tf_op jit(solution)/shard_map/dynamic_slice | solution.py:154
  8.3 4.6 %collective-permute-start.5 = (bf16[256,1024]{1,0:T(8,128)(2,1)S(1)}, bf16[256,1024]{1,0:T(8,128)(2,1)S(1)}, u32[]{:S(2)}, u32[]{:S(2)}) collective-permute-start(bf16[256,1024]{1,0:T(8,128)(2,1)S(1)} %constant_dynamic-slice_fusion), channel_id=1, source_target_pairs={{0,2},{2,4},{4,6},{6,8},{8,10},{10,12},{12,14},{14,16},{16,18},{18... | collective-permute-start | bytes 1572872 | tf_op jit(solution)/shard_map/ppermute | solution.py:23
  12.9 0.0 copy-done.14
  12.9 0.0 copy-done.12
  13.0 0.0 copy-done.13
  13.0 0.0 copy-done
  13.0 7.6 %shard_map.145 = (bf16[1024,512]{1,0:T(8,128)(2,1)S(1)}, bf16[1024,512]{1,0:T(8,128)(2,1)S(1)}, bf16[1024,512]{1,0:T(8,128)(2,1)S(1)}, bf16[1024,512]{1,0:T(8,128)(2,1)S(1)}) custom-call(bf16[1024,1024]{1,0:T(8,128)(2,1)} %stream.1, bf16[1,1024]{1,0:T(2,128)(2,1)S(1)} %broadcast_in_dim.15.gain, bf16[1024,512]{1,0:T(8,128)(2,1)S(1)} %copy-done, ...), custom_call_target="tpu_custom_call" | custom-call | flops 4294967296 | bytes 12582912 | tf_op jit(solution)/shard_map/pallas_call | solution.py:163
  20.6 0.0 copy-start.7
  20.6 1.0 %copy-done.7 = bf16[1024,512]{1,0:T(8,128)(2,1)} copy-done((bf16[1024,512]{1,0:T(8,128)(2,1)}, bf16[1024,512]{1,0:T(8,128)(2,1)S(1)}, u32[]{:S(2)}) %copy-start.7) | copy-done | bytes 1048600
  21.6 0.0 copy-start.9
  21.6 1.0 %copy-done.9 = bf16[1024,512]{1,0:T(8,128)(2,1)} copy-done((bf16[1024,512]{1,0:T(8,128)(2,1)}, bf16[1024,512]{1,0:T(8,128)(2,1)S(1)}, u32[]{:S(2)}) %copy-start.9) | copy-done | bytes 1048600
  22.6 0.0 copy-start.3
  22.6 0.0 copy-start.5
  22.6 2.0 %collective-permute-done.5.mine = bf16[256,1024]{1,0:T(8,128)(2,1)S(1)} collective-permute-done((bf16[256,1024]{1,0:T(8,128)(2,1)S(1)}, bf16[256,1024]{1,0:T(8,128)(2,1)S(1)}, u32[]{:S(2)}, u32[]{:S(2)}) %collective-permute-start.5) | collective-permute-done | bytes 524320 | tf_op jit(solution)/shard_map/ppermute | solution.py:23
  24.5 0.0 collective-permute-start.6
  24.5 0.0 collective-permute-done.1
  24.5 1.4 %add_convert_fusion.1.rep = bf16[256,1024]{1,0:T(8,128)(2,1)S(1)} fusion(f32[256,1024]{1,0:T(8,128)S(1)} %fusion.3, f32[256,1024]{1,0:T(8,128)} %collective-permute-done.1), kind=kLoop, calls=%fused_computation.7 | loop fusion | flops 524288 | bytes 2621440 | tf_op jit(solution)/shard_map/convert_element_type | solution.py:178
  25.9 4.4 %collective-permute-start.2 = (bf16[160,512]{1,0:T(8,128)(2,1)S(1)}, bf16[160,512]{1,0:T(8,128)(2,1)S(1)}, u32[]{:S(2)}, u32[]{:S(2)}) collective-permute-start(bf16[160,512]{1,0:T(8,128)(2,1)S(1)} %dynamic-slice), channel_id=1, source_target_pairs={{0,2},{2,4},{4,6},{6,8},{8,10},{10,12},{12,14},{14,16},{16,18},{18... | collective-permute-start | bytes 491528 | tf_op jit(solution)/shard_map/ppermute | solution.py:23
  30.4 1.3 %collective-permute-start.3 = (bf16[32,512]{1,0:T(8,128)(2,1)S(1)}, bf16[32,512]{1,0:T(8,128)(2,1)S(1)}, u32[]{:S(2)}, u32[]{:S(2)}) collective-permute-start(bf16[32,512]{1,0:T(8,128)(2,1)S(1)} %constant_dynamic-slice_fusion.1), channel_id=1, source_target_pairs={{2,0},{4,2},{6,4},{8,6},{10,8},{12,10},{14,12},{16,14},{18,16},{20... | collective-permute-start | bytes 98312 | tf_op jit(solution)/shard_map/ppermute | solution.py:23
  31.7 0.1 fusion.7
  31.7 0.0 copy-done.3
  31.7 0.0 copy-done.5
  31.7 0.2 copy.16.low_key
  32.0 0.2 copy.17.low_key
  32.2 5.8 %collective-permute-done.3.right_mine = bf16[32,512]{1,0:T(8,128)(2,1)S(1)} collective-permute-done((bf16[32,512]{1,0:T(8,128)(2,1)S(1)}, bf16[32,512]{1,0:T(8,128)(2,1)S(1)}, u32[]{:S(2)}, u32[]{:S(2)}) %collective-permute-start.3) | collective-permute-done | bytes 32800 | tf_op jit(solution)/shard_map/ppermute | solution.py:23
  38.0 0.0 collective-permute-done.2.left_mine
  38.0 0.1 collective-permute-start.4
  38.1 0.0 collective-permute-done.6.other
  38.1 0.0 copy-start.6
  38.1 1.2 %copy-done.6 = bf16[1024,512]{1,0:T(8,128)(2,1)S(1)} copy-done((bf16[1024,512]{1,0:T(8,128)(2,1)S(1)}, bf16[1024,512]{1,0:T(8,128)(2,1)}, u32[]{:S(2)}) %copy-start.6) | copy-done | bytes 1048600
  39.3 0.0 copy-start.8
  39.3 1.2 %copy-done.8 = bf16[1024,512]{1,0:T(8,128)(2,1)S(1)} copy-done((bf16[1024,512]{1,0:T(8,128)(2,1)S(1)}, bf16[1024,512]{1,0:T(8,128)(2,1)}, u32[]{:S(2)}) %copy-start.8) | copy-done | bytes 1048600
  40.5 0.0 copy-start.10
  40.6 1.2 %copy-done.10 = bf16[1024,512]{1,0:T(8,128)(2,1)S(1)} copy-done((bf16[1024,512]{1,0:T(8,128)(2,1)S(1)}, bf16[1024,512]{1,0:T(8,128)(2,1)}, u32[]{:S(2)}) %copy-start.10) | copy-done | bytes 1048600
  41.8 0.0 copy-start.1
  41.8 0.0 copy-start.2
  41.8 0.0 copy-start.4
  41.8 14.4 %shard_map.146.mixed = bf16[1024,512]{1,0:T(8,128)(2,1)S(1)} custom-call(bf16[1024,512]{1,0:T(8,128)(2,1)S(1)} %copy-done.10, bf16[1024,512]{1,0:T(8,128)(2,1)S(1)} %copy-done.6, bf16[1024,512]{1,0:T(8,128)(2,1)S(1)} %copy-done.8, bf16[256,1024]{1,0:T(8,128)(2,1)S(1)} %collective-permute-done.5.mine, bf16[256,1024]{1,0:T(8,128)(2,1)S(1)} %collective-permute-done.6.other, ...), custom_call_target="tpu_custom_call" | custom-call | flops 17179869184 | bytes 6291456 | tf_op jit(solution)/shard_map/pallas_call | solution.py:190
  56.2 0.0 copy-start.11
  56.2 1.0 %copy-done.11 = bf16[1024,512]{1,0:T(8,128)(2,1)} copy-done((bf16[1024,512]{1,0:T(8,128)(2,1)}, bf16[1024,512]{1,0:T(8,128)(2,1)S(1)}, u32[]{:S(2)}) %copy-start.11) | copy-done | bytes 1048600
  57.2 0.0 collective-permute-done.4
  57.2 0.0 copy-done.1
  57.2 0.0 copy-done.2
  57.2 0.0 copy-done.4
  57.2 13.0 %shard_map.147 = (f32[1024,512]{1,0:T(8,128)}, bf16[1024,512]{1,0:T(8,128)(2,1)S(1)}) custom-call(bf16[1024,512]{1,0:T(8,128)(2,1)S(1)} %copy-done.4, bf16[256,1024]{1,0:T(8,128)(2,1)S(1)} %add_convert_fusion.1.rep, bf16[160,512]{1,0:T(8,128)(2,1)S(1)} %collective-permute-done.2.left_mine, bf16[160,512]{1,0:T(8,128)(2,1)S(1)} %slice.16.left_other, ...), custom_call_target="tpu_custom_call" | custom-call | flops 10737418240 | bytes 8388608 | tf_op jit(solution)/shard_map/pallas_call | solution.py:211
  70.2 0.5 collective-permute-start.7
  70.7 2.3 %collective-permute-done.7 = bf16[1024,512]{1,0:T(8,128)(2,1)S(1)} collective-permute-done((bf16[1024,512]{1,0:T(8,128)(2,1)S(1)}, bf16[1024,512]{1,0:T(8,128)(2,1)S(1)}, u32[]{:S(2)}, u32[]{:S(2)}) %collective-permute-start.7) | collective-permute-done | bytes 1048608 | tf_op jit(solution)/shard_map/ppermute | solution.py:27
  73.0 2.9 %add_convert_fusion = bf16[1024,512]{1,0:T(8,128)(2,1)} fusion(f32[1024,512]{1,0:T(8,128)} %get-tuple-element.15, bf16[1024,512]{1,0:T(8,128)(2,1)S(1)} %collective-permute-done.7), kind=kLoop, calls=%fused_computation.5 | loop fusion | flops 1572864 | bytes 4194304 | tf_op jit(solution)/shard_map/convert_element_type | solution.py:231
  (9 shorter events, 0.1 us)
Async XLA Ops:
  1.5 1.4 %collective-permute-start = (f32[256]{0:T(256)S(1)}, f32[256]{0:T(256)S(1)}, u32[]{:S(2)}, u32[]{:S(2)}) collective-permute-start(f32[256]{0:T(256)S(1)} %fusion), channel_id=1, source_target_pairs={{0,1},{1,0},{2,3},{3,2},{4,5},{5,4},{6,7},{7,6},{8,9},{9,8},{10,11... | collective-permute-start | bytes 3080 | tf_op jit(solution)/shard_map/ppermute | solution.py:27
  2.9 10.0 %copy-start.14 = (bf16[1024]{0:T(1024)(128)(2,1)S(1)}, bf16[1024]{0:T(1024)(128)(2,1)}, u32[]{:S(2)}) copy-start(bf16[1024]{0:T(1024)(128)(2,1)} %param.21) | copy-start | bytes 6148
  2.9 10.0 %copy-start.12 = (s32[4096]{0:T(1024)S(1)}, s32[4096]{0:T(1024)}, u32[]{:S(2)}) copy-start(s32[4096]{0:T(1024)} %param.18) | copy-start | bytes 49156
  2.9 10.1 %copy-start.13 = (s32[1024]{0:T(1024)S(1)}, s32[1024]{0:T(1024)}, u32[]{:S(2)}) copy-start(s32[1024]{0:T(1024)} %param.20) | copy-start | bytes 12292
  2.9 10.1 %copy-start = (bf16[1024,512]{1,0:T(8,128)(2,1)S(1)}, bf16[1024,512]{1,0:T(8,128)(2,1)}, u32[]{:S(2)}) copy-start(bf16[1024,512]{1,0:T(8,128)(2,1)} %wk.4) | copy-start | bytes 3145732
  6.8 17.7 %collective-permute-start.1 = (f32[256,1024]{1,0:T(8,128)S(1)}, f32[256,1024]{1,0:T(8,128)}, u32[]{:S(2)}, u32[]{:S(2)}) collective-permute-start(f32[256,1024]{1,0:T(8,128)S(1)} %fusion.3), channel_id=1, source_target_pairs={{0,1},{1,0},{2,3},{3,2},{4,5},{5,4},{6,7},{7,6},{8,9},{9,8},{10,11... | collective-permute-start | bytes 3145736 | tf_op jit(solution)/shard_map/ppermute | solution.py:27
  8.3 16.2 %collective-permute-start.5 = (bf16[256,1024]{1,0:T(8,128)(2,1)S(1)}, bf16[256,1024]{1,0:T(8,128)(2,1)S(1)}, u32[]{:S(2)}, u32[]{:S(2)}) collective-permute-start(bf16[256,1024]{1,0:T(8,128)(2,1)S(1)} %constant_dynamic-slice_fusion), channel_id=1, source_target_pairs={{0,2},{2,4},{4,6},{6,8},{8,10},{10,12},{12,14},{14,16},{16,18},{18... | collective-permute-start | bytes 1572872 | tf_op jit(solution)/shard_map/ppermute | solution.py:23
  20.6 1.0 %copy-start.7 = (bf16[1024,512]{1,0:T(8,128)(2,1)}, bf16[1024,512]{1,0:T(8,128)(2,1)S(1)}, u32[]{:S(2)}) copy-start(bf16[1024,512]{1,0:T(8,128)(2,1)S(1)} %get-tuple-element.14.v) | copy-start | bytes 3145732
  21.6 1.0 %copy-start.9 = (bf16[1024,512]{1,0:T(8,128)(2,1)}, bf16[1024,512]{1,0:T(8,128)(2,1)S(1)}, u32[]{:S(2)}) copy-start(bf16[1024,512]{1,0:T(8,128)(2,1)S(1)} %get-tuple-element.12.q) | copy-start | bytes 3145732
  22.6 9.2 %copy-start.3 = (bf16[1024,512]{1,0:T(8,128)(2,1)}, bf16[1024,512]{1,0:T(8,128)(2,1)S(1)}, u32[]{:S(2)}) copy-start(bf16[1024,512]{1,0:T(8,128)(2,1)S(1)} %get-tuple-element.11.q) | copy-start | bytes 3145732
  22.6 9.2 %copy-start.5 = (bf16[1024,512]{1,0:T(8,128)(2,1)}, bf16[1024,512]{1,0:T(8,128)(2,1)S(1)}, u32[]{:S(2)}) copy-start(bf16[1024,512]{1,0:T(8,128)(2,1)S(1)} %get-tuple-element.13.k) | copy-start | bytes 3145732
  24.5 13.6 %collective-permute-start.6 = (bf16[256,1024]{1,0:T(8,128)(2,1)S(1)}, bf16[256,1024]{1,0:T(8,128)(2,1)S(1)}, u32[]{:S(2)}, u32[]{:S(2)}) collective-permute-start(bf16[256,1024]{1,0:T(8,128)(2,1)S(1)} %collective-permute-done.5.mine), channel_id=1, source_target_pairs={{0,1},{1,0},{2,3},{3,2},{4,5},{5,4},{6,7},{7,6},{8,9},{9,8},{10,11... | collective-permute-start | bytes 1572872 | tf_op jit(solution)/shard_map/ppermute | solution.py:27
  25.9 12.1 %collective-permute-start.2 = (bf16[160,512]{1,0:T(8,128)(2,1)S(1)}, bf16[160,512]{1,0:T(8,128)(2,1)S(1)}, u32[]{:S(2)}, u32[]{:S(2)}) collective-permute-start(bf16[160,512]{1,0:T(8,128)(2,1)S(1)} %dynamic-slice), channel_id=1, source_target_pairs={{0,2},{2,4},{4,6},{6,8},{8,10},{10,12},{12,14},{14,16},{16,18},{18... | collective-permute-start | bytes 491528 | tf_op jit(solution)/shard_map/ppermute | solution.py:23
  30.4 7.6 %collective-permute-start.3 = (bf16[32,512]{1,0:T(8,128)(2,1)S(1)}, bf16[32,512]{1,0:T(8,128)(2,1)S(1)}, u32[]{:S(2)}, u32[]{:S(2)}) collective-permute-start(bf16[32,512]{1,0:T(8,128)(2,1)S(1)} %constant_dynamic-slice_fusion.1), channel_id=1, source_target_pairs={{2,0},{4,2},{6,4},{8,6},{10,8},{12,10},{14,12},{16,14},{18,16},{20... | collective-permute-start | bytes 98312 | tf_op jit(solution)/shard_map/ppermute | solution.py:23
  38.0 19.2 %collective-permute-start.4 = (bf16[192,512]{1,0:T(8,128)(2,1)S(1)}, bf16[192,512]{1,0:T(8,128)(2,1)S(1)}, u32[]{:S(2)}, u32[]{:S(2)}) collective-permute-start(bf16[192,512]{1,0:T(8,128)(2,1)S(1)} %pad_maximum_fusion), channel_id=1, source_target_pairs={{0,1},{1,0},{2,3},{3,2},{4,5},{5,4},{6,7},{7,6},{8,9},{9,8},{10,11... | collective-permute-start | bytes 589832 | tf_op jit(solution)/shard_map/ppermute | solution.py:27
  38.1 1.2 %copy-start.6 = (bf16[1024,512]{1,0:T(8,128)(2,1)S(1)}, bf16[1024,512]{1,0:T(8,128)(2,1)}, u32[]{:S(2)}) copy-start(bf16[1024,512]{1,0:T(8,128)(2,1)} %copy-done.5) | copy-start | bytes 3145732
  39.3 1.2 %copy-start.8 = (bf16[1024,512]{1,0:T(8,128)(2,1)S(1)}, bf16[1024,512]{1,0:T(8,128)(2,1)}, u32[]{:S(2)}) copy-start(bf16[1024,512]{1,0:T(8,128)(2,1)} %copy-done.7) | copy-start | bytes 3145732
  40.5 1.2 %copy-start.10 = (bf16[1024,512]{1,0:T(8,128)(2,1)S(1)}, bf16[1024,512]{1,0:T(8,128)(2,1)}, u32[]{:S(2)}) copy-start(bf16[1024,512]{1,0:T(8,128)(2,1)} %copy-done.9) | copy-start | bytes 3145732
  41.8 15.4 %copy-start.1 = (bf16[1024,512]{1,0:T(8,128)(2,1)S(1)}, bf16[1024,512]{1,0:T(8,128)(2,1)}, u32[]{:S(2)}) copy-start(bf16[1024,512]{1,0:T(8,128)(2,1)} %wk.5) | copy-start | bytes 3145732
  41.8 15.4 %copy-start.2 = (bf16[1024,512]{1,0:T(8,128)(2,1)S(1)}, bf16[1024,512]{1,0:T(8,128)(2,1)}, u32[]{:S(2)}) copy-start(bf16[1024,512]{1,0:T(8,128)(2,1)} %wv.5) | copy-start | bytes 3145732
  41.8 15.5 %copy-start.4 = (bf16[1024,512]{1,0:T(8,128)(2,1)S(1)}, bf16[1024,512]{1,0:T(8,128)(2,1)}, u32[]{:S(2)}) copy-start(bf16[1024,512]{1,0:T(8,128)(2,1)} %copy-done.3) | copy-start | bytes 3145732
  56.2 1.0 %copy-start.11 = (bf16[1024,512]{1,0:T(8,128)(2,1)}, bf16[1024,512]{1,0:T(8,128)(2,1)S(1)}, u32[]{:S(2)}) copy-start(bf16[1024,512]{1,0:T(8,128)(2,1)S(1)} %shard_map.146.mixed) | copy-start | bytes 3145732
  70.2 2.8 %collective-permute-start.7 = (bf16[1024,512]{1,0:T(8,128)(2,1)S(1)}, bf16[1024,512]{1,0:T(8,128)(2,1)S(1)}, u32[]{:S(2)}, u32[]{:S(2)}) collective-permute-start(bf16[1024,512]{1,0:T(8,128)(2,1)S(1)} %get-tuple-element.16), channel_id=1, source_target_pairs={{0,1},{1,0},{2,3},{3,2},{4,5},{5,4},{6,7},{7,6},{8,9},{9,8},{10,11... | collective-permute-start | bytes 3145736 | tf_op jit(solution)/shard_map/ppermute | solution.py:27

commit v2 on v0

--- a/solution.py
+++ b/solution.py
@@ -1,25 +1,54 @@
 import jax
 import jax.numpy as jnp
 from jax import lax
+from jax.experimental import pallas as pl
+from jax.experimental.pallas import tpu as pltpu
 from jax.sharding import PartitionSpec as P
 
 HD = 64
 WIN = 512
 PMAX = 448
+DRIFT = 32
+LANES = 128
+QB = 256
+F32 = jnp.float32
+BF16 = jnp.bfloat16
+FAR = -1e30
+MESH = pl.DeviceIdType.MESH
+
+
+def norm_rows(values, gain):
+    widened = values.astype(F32)
+    mean_square = jnp.mean(widened * widened, axis=1, keepdims=True)
+    return (widened * lax.rsqrt(mean_square + 1e-05) * gain.astype(F32)).astype(BF16)
+
+
+def mm(left, right):
+    return jnp.dot(left, right, preferred_element_type=F32)
+
+
+def pair_attend(query, keys, values, bias):
+    rows = query.shape[0]
+    low = lax.broadcasted_iota(jnp.int32, (rows, LANES), 1) < HD
+    zero = jnp.zeros_like(query)
+    scaled = query * jnp.asarray(HD**-0.5, BF16)
+    both = jnp.concatenate([jnp.where(low, scaled, zero), jnp.where(low, zero, scaled)], axis=0)
+    scores = lax.dot_general(both, keys, (((1,), (1,)), ((), ())), preferred_element_type=F32)
+    wide = jnp.concatenate([values, jnp.ones_like(values)], axis=1)
+    mixed = []
+    for half in range(2):
+        one = scores[half * rows : (half + 1) * rows] + bias
+        top = jnp.max(one, axis=1, keepdims=True)
+        weights = jnp.exp(one - top).astype(BF16)
+        total = mm(weights, wide)
+        mixed.append(total[:, :LANES] / total[:, LANES:])
+    return jnp.where(low, mixed[0], mixed[1]).astype(BF16)
 
 
 def from_behind(array, axis, by):
     devices = lax.axis_size(axis)
     pairs = [(i, i + by) for i in range(devices) if 0 <= i + by < devices]
     return lax.ppermute(array, axis, pairs)
-
-
-def norm_rows(values, gain):
-    widened = values.astype(jnp.float32)
-    mean_square = jnp.mean(widened * widened, axis=1, keepdims=True)
-    return (widened * lax.rsqrt(mean_square + 1e-05) * gain.astype(jnp.float32)).astype(
-        jnp.bfloat16
-    )
 
 
 def project(left, right):
@@ -45,7 +74,7 @@
     return head_mix.reshape(row_count, head_count * head_size).astype(jnp.bfloat16)
 
 
-def on_device(
+def general_device(
     latent,
     latent_gain,
     proj_weight,
@@ -127,25 +156,275 @@
     return lax.psum_scatter(partial_out.astype(jnp.bfloat16), "tp", scatter_dimension=1, tiled=True)
 
 
+def layer_kernel(
+    latent_h, proj_h, stream_h, wk_h, wv_h, wq_h, wc_h, ck_h, cv_h, so_h, co_h,
+    latent_gain, gain, starts, low_key, out,
+    latent, proj, stream, wk, wv, wq, wc, ck, cv, so, co,
+    halo, keys, values, queries, cross_rows, mixed, cross, sq_mine, sq_peer, part_mine, part_peer,
+    joined, patch_keys, patch_values, own, far, far_peer, local_sem, send_sem, recv_sem,
+):
+    seg, width = stream.shape
+    cols = wk.shape[1]
+    patch_dev = latent.shape[0]
+    place, place_seq = lax.axis_index("tp"), lax.axis_index("seq")
+    last = lax.axis_size("seq") - 1
+    peer = {"tp": 1 - place}
+    right, left = {"seq": jnp.minimum(place_seq + 1, last)}, {"seq": jnp.maximum(place_seq - 1, 0)}
+    has_left, has_right = place_seq > 0, place_seq < last
+    here = pl.ds(pl.multiple_of(place * cols, cols), cols)
+    there = pl.ds(pl.multiple_of((1 - place) * cols, cols), cols)
+
+    pairs = (
+        (latent_h, latent), (stream_h, stream), (wk_h, wk), (wv_h, wv), (wq_h, wq), (wc_h, wc),
+        (proj_h, proj), (ck_h, ck), (cv_h, cv), (so_h, so), (co_h, co),
+    )
+    loads = [pltpu.make_async_copy(a, b, local_sem.at[i]) for i, (a, b) in enumerate(pairs)]
+    for load in loads:
+        load.start()
+
+    barrier = pltpu.get_barrier_semaphore()
+    pl.semaphore_signal(barrier, inc=1, device_id=peer, device_id_type=MESH)
+
+    @pl.when(has_left)
+    def _():
+        pl.semaphore_signal(barrier, inc=1, device_id=left, device_id_type=MESH)
+
+    @pl.when(has_right)
+    def _():
+        pl.semaphore_signal(barrier, inc=1, device_id=right, device_id_type=MESH)
+
+    pl.semaphore_wait(barrier, 1 + has_left.astype(jnp.int32) + has_right.astype(jnp.int32))
+
+    def send(source, target, index, to):
+        return pltpu.make_async_remote_copy(
+            src_ref=source, dst_ref=target, send_sem=send_sem.at[index], recv_sem=recv_sem.at[index],
+            device_id=to, device_id_type=MESH,
+        )
+
+    half = WIN // 2
+    mine = pl.ds(pl.multiple_of(place * half, half), half)
+    tail = pl.ds(pl.multiple_of(seg - WIN + place * half, half), half)
+    halo_send = send(stream_h.at[tail, :], halo.at[mine, :], 0, right)
+    halo_swap = send(halo.at[mine, :], halo.at[mine, :], 1, peer)
+    sq_swap = send(sq_mine, sq_peer, 2, peer)
+    part_swap = send(part_mine, part_peer, 3, peer)
+    after = DRIFT
+    before = joined.shape[0] - patch_dev - after
+    front, back = pl.ds(0, before), pl.ds(before + patch_dev, after)
+    rep_right = send(joined.at[pl.ds(patch_dev, before), here], joined.at[front, here], 4, right)
+    rep_left = send(joined.at[pl.ds(before, after), here], joined.at[back, here], 5, left)
+    front_swap = send(joined.at[front, here], joined.at[front, here], 6, peer)
+    back_swap = send(joined.at[back, here], joined.at[back, here], 7, peer)
+
+    @pl.when(has_right)
+    def _():
+        halo_send.start()
+
+    loads[0].wait()
+    widened = latent[...].astype(F32)
+    square = jnp.sum(widened * widened, axis=1, keepdims=True)
+    sq_mine[...] = jnp.broadcast_to(square, sq_mine.shape)
+    sq_swap.start()
+
+    for load in loads[1:6]:
+        load.wait()
+
+    def project_rows(step, carry):
+        rows = pl.ds(pl.multiple_of(step * QB, QB), QB)
+        shifted = pl.ds(pl.multiple_of(step * QB + WIN, QB), QB)
+        hidden = norm_rows(stream[rows, :], gain[...])
+        keys[shifted, :] = mm(hidden, wk[...]).astype(BF16)
+        values[shifted, :] = mm(hidden, wv[...]).astype(BF16)
+        queries[rows, :] = mm(hidden, wq[...]).astype(BF16)
+        cross_rows[rows, :] = mm(hidden, wc[...]).astype(BF16)
+        return carry
+
+    lax.fori_loop(0, seg // QB, project_rows, 0)
+
+    loads[6].wait()
+    sq_swap.wait()
+    scale = lax.rsqrt((sq_mine[:, :1] + sq_peer[:, :1]) / (2 * latent.shape[1]) + 1e-05)
+    normed = (latent[...].astype(F32) * scale * latent_gain[...].astype(F32)).astype(BF16)
+    part_mine[...] = mm(normed, proj[...])
+    part_swap.start()
+
+    count = WIN + QB
+    index = lax.broadcasted_iota(jnp.int32, (QB, count), 1)
+    row = lax.broadcasted_iota(jnp.int32, (QB, count), 0)
+
+    def self_rows(step, carry):
+        base = pl.multiple_of(step * QB, QB)
+        rows, near = pl.ds(base, QB), pl.ds(base, count)
+        allowed = (index <= row + WIN) & (index >= low_key[rows, :] + (WIN - base))
+        bias = jnp.where(allowed, 0.0, FAR).astype(F32)
+        for col in range(0, cols, LANES):
+            at = slice(col, col + LANES)
+            mixed[rows, at] = pair_attend(queries[rows, at], keys[near, at], values[near, at], bias)
+        return carry
+
+    inner = WIN // QB
+    lax.fori_loop(inner, inner + 1, self_rows, 0)
+
+    part_swap.wait()
+    joined[pl.ds(before, patch_dev), :] = (part_mine[...] + part_peer[...]).astype(BF16)
+
+    @pl.when(has_right)
+    def _():
+        rep_right.start()
+        halo_send.wait_send()
+
+    @pl.when(has_left)
+    def _():
+        rep_left.start()
+        halo_send.wait_recv()
+        halo_swap.start()
+
+    lax.fori_loop(inner + 1, seg // QB, self_rows, 0)
+
+    @pl.when(has_right)
+    def _():
+        rep_right.wait_send()
+        rep_left.wait_recv()
+        back_swap.start()
+
+    @pl.when(has_left)
+    def _():
+        rep_left.wait_send()
+        rep_right.wait_recv()
+        front_swap.start()
+        halo_swap.wait()
+
+    @pl.when(jnp.logical_not(has_left))
+    def _():
+        halo[...] = jnp.zeros_like(halo)
+        joined[front, :] = jnp.zeros((before, width), BF16)
+
+    @pl.when(jnp.logical_not(has_right))
+    def _():
+        joined[back, :] = jnp.zeros((after, width), BF16)
+
+    hidden = norm_rows(halo[...], gain[...])
+    keys[:WIN, :] = mm(hidden, wk[...]).astype(BF16)
+    values[:WIN, :] = mm(hidden, wv[...]).astype(BF16)
+    lax.fori_loop(0, inner, self_rows, 0)
+
+    @pl.when(has_right)
+    def _():
+        back_swap.wait()
+
+    @pl.when(has_left)
+    def _():
+        front_swap.wait()
+
+    for load in loads[7:]:
+        load.wait()
+    used = joined.shape[0]
+    for weight, target in ((ck, patch_keys), (cv, patch_values)):
+        target[:used, :] = mm(joined[...], weight[...]).astype(BF16)
+        target[used:, :] = jnp.zeros((target.shape[0] - used, cols), BF16)
+
+    slots = patch_keys.shape[0] - LANES
+    slot_row = lax.broadcasted_iota(jnp.int32, (QB, slots), 0)
+
+    def out_swap(step):
+        rows = pl.ds(pl.multiple_of(step * QB, QB), QB)
+        return send(far.at[rows, :], far_peer.at[rows, :], 8 + step, peer)
+
+    def finish(step):
+        out_swap(step).wait()
+        rows = pl.ds(pl.multiple_of(step * QB, QB), QB)
+        out[rows, :] = (own[rows, :] + far_peer[rows, :].astype(F32)).astype(BF16)
+
+    def cross_block(step, carry):
+        rows = pl.ds(pl.multiple_of(step * QB, QB), QB)
+        base = pl.multiple_of(lax.rem(lax.div(step, inner), 2) * LANES, LANES)
+        near = pl.ds(base, slots)
+        first = starts[:, near]
+        allowed = (first <= slot_row + step * QB) & (first >= low_key[rows, :])
+        bias = jnp.where(allowed, 0.0, FAR).astype(F32)
+        for col in range(0, cols, LANES):
+            at = slice(col, col + LANES)
+            cross[:, at] = pair_attend(
+                cross_rows[rows, at], patch_keys[near, at], patch_values[near, at], bias
+            )
+        far[rows, :] = (mm(mixed[rows, :], so[:, there]) + mm(cross[...], co[:, there])).astype(BF16)
+        out_swap(step).start()
+        own[rows, :] = mm(mixed[rows, :], so[:, here]) + mm(cross[...], co[:, here])
+
+        @pl.when(step > 0)
+        def _():
+            finish(step - 1)
+
+        return carry
+
+    lax.fori_loop(0, seg // QB, cross_block, 0)
+    finish(seg // QB - 1)
+
+
+def pair_device(
+    latent, latent_gain, proj_weight, patch_starts, stream, doc_starts, stream_gain,
+    self_query, self_key, self_value, self_out, cross_query, cross_key, cross_value, cross_out,
+):
+    seg, width = stream.shape
+    patch_dev, features = latent.shape
+    cols = self_query.shape[1]
+    first_byte = lax.axis_index("seq") * seg
+    before, after = WIN * patch_dev // seg + DRIFT, DRIFT
+    used = before + patch_dev + after
+    slots = (used + LANES - 1) // LANES * LANES
+
+    positions = jnp.arange(seg, dtype=jnp.int32)
+    low_byte = jnp.maximum(positions - WIN, doc_starts - first_byte)[:, None]
+    padded = jnp.pad(
+        patch_starts - first_byte, (before, slots), constant_values=seg * (lax.axis_size("seq") + 1)
+    )
+    window = lax.dynamic_slice_in_dim(padded, lax.axis_index("seq") * patch_dev, slots, 0)
+    window = jnp.where(jnp.arange(slots) < used, window, seg)[None, :]
+
+    big = (latent, proj_weight, stream, self_key, self_value, self_query, cross_query, cross_key, cross_value, self_out, cross_out)
+    small = (latent_gain[None, :], stream_gain[None, :], window, low_byte)
+    blocks = seg // QB
+    return pl.pallas_call(
+        layer_kernel,
+        in_specs=[pl.BlockSpec(memory_space=pl.ANY)] * len(big)
+        + [pl.BlockSpec(memory_space=pltpu.VMEM)] * len(small),
+        out_specs=pl.BlockSpec(memory_space=pltpu.VMEM),
+        out_shape=jax.ShapeDtypeStruct((seg, cols), BF16),
+        scratch_shapes=[pltpu.VMEM(array.shape, BF16) for array in big]
+        + [
+            pltpu.VMEM((WIN, width), BF16),
+            pltpu.VMEM((WIN + seg, cols), BF16),
+            pltpu.VMEM((WIN + seg, cols), BF16),
+            pltpu.VMEM((seg, cols), BF16),
+            pltpu.VMEM((seg, cols), BF16),
+            pltpu.VMEM((seg, cols), BF16),
+            pltpu.VMEM((QB, cols), BF16),
+            pltpu.VMEM((patch_dev, LANES), F32),
+            pltpu.VMEM((patch_dev, LANES), F32),
+            pltpu.VMEM((patch_dev, width), F32),
+            pltpu.VMEM((patch_dev, width), F32),
+            pltpu.VMEM((used, width), BF16),
+            pltpu.VMEM((slots, cols), BF16),
+            pltpu.VMEM((slots, cols), BF16),
+            pltpu.VMEM((seg, cols), F32),
+            pltpu.VMEM((seg, cols), BF16),
+            pltpu.VMEM((seg, cols), BF16),
+            pltpu.SemaphoreType.DMA((len(big),)),
+            pltpu.SemaphoreType.DMA((8 + blocks,)),
+            pltpu.SemaphoreType.DMA((8 + blocks,)),
+        ],
+        compiler_params=pltpu.CompilerParams(
+            collective_id=0, has_side_effects=True, vmem_limit_bytes=60 << 20
+        ),
+    )(*big, *small)
+
+
 def solution(mesh):
     in_specs = (
-        P("seq", "tp"),
-        P("tp"),
-        P("tp", None),
-        P(),
-        P("seq", None),
-        P("seq"),
-        P(),
-        P(None, "tp"),
-        P(None, "tp"),
-        P(None, "tp"),
-        P("tp", None),
-        P(None, "tp"),
-        P(None, "tp"),
-        P(None, "tp"),
-        P("tp", None),
-    )
-    out_specs = P("seq", "tp")
+        P("seq", "tp"), P("tp"), P("tp", None), P(), P("seq", None), P("seq"), P(),
+        P(None, "tp"), P(None, "tp"), P(None, "tp"), P("tp", None),
+        P(None, "tp"), P(None, "tp"), P(None, "tp"), P("tp", None),
+    )
     return jax.shard_map(
-        on_device, mesh=mesh, in_specs=in_specs, out_specs=out_specs, check_vma=False
-    )
+        pair_device if mesh.shape["tp"] == 2 else general_device, mesh=mesh, in_specs=in_specs, out_specs=P("seq", "tp"), check_vma=False
+    )

time: 160 us -> 50.7 us (0.32)
  matrix products: 91.1 us -> 0 us
  Pallas kernels: 0 us -> 42.4 us
  waiting for transfers between devices: 19.1 us -> 0 us
  between operations: 14.3 us -> 0.01 us
  starting transfers between devices: 9.86 us -> 0 us
  other arithmetic: 11.8 us -> 2.05 us
  blocking collectives: 4.93 us -> 0 us
  local copies, waits for them, and re-layouts: 8.5 us -> 5.85 us
    dot_general x11 -> x0, matrix products: 51.7 us -> none  [the longest x2 24.9 us: attend(): jnp.einsum('hrk,khd->rhd', probs, value_heads, preferred_element_type=jnp...]
    pallas_call x0 -> x1, Pallas kernels: none -> 42.4 us  [pair_device(): pl.pallas_call(layer_kernel, in_specs=[pl.BlockSpec(memory_space=pl.ANY)]...]
    sub x2 -> x0, matrix products: 39.4 us -> none  [attend(): weights = jnp.where(allowed[None], jnp.exp(scores - row_max), 0.0)]
    reduce_scatter x2 -> x0, waiting for transfers between devices: 10.4 us -> none  [the longest x1 10.4 us: on_device(): lax.psum_scatter(partial_out.astype(jnp.bfloat16), 'tp', scatter_dimensio...]
    ppermute x3 -> x0, starting transfers between devices: 9.82 us -> none  [from_behind(): return lax.ppermute(array, axis, pairs)]
    ppermute x3 -> x0, waiting for transfers between devices: 8.62 us -> none  [from_behind(): return lax.ppermute(array, axis, pairs)]
    broadcast_in_dim x0 -> x3, local copies, waits for them, and re-layouts: none -> 3.58 us  [the longest x2 2.56 us: pair_device(): small = (latent_gain[None, :], stream_gain[None, :], window, low_byte)]
    and x2 -> x0, other arithmetic: 3.45 us -> none  [the longest x1 2.13 us: on_device(): (key_pos[None, :] <= positions[:, None]) & (key_pos[None, :] >= positions...]
  transfers between devices with their start and end apart: 5 -> 0, of which waited for: 3 -> 0; matrix products, arithmetic and copies ran while one was open for 46% -> 0% of each run, Pallas kernels for 0% -> 0%
where the time goes in v2:
time: 50.7 us; the launch traced here: 50.3 us
  Pallas kernels  42.4 us (84%)
  local copies, waits for them, and re-layouts  5.85 us (12%)
  other arithmetic  2.05 us (4%)
    pallas_call x1, Pallas kernels, pair_device(): pl.pallas_call(layer_kernel, in_specs=[pl.BlockSpec(memory_space=pl.ANY)]...  42.4 us
    broadcast_in_dim x2, local copies, waits for them, and re-layouts, pair_device(): small = (latent_gain[None, :], stream_gain[None, :], window, low_byte)  2.56 us
    unnamed x1, local copies, waits for them, and re-layouts  2.26 us
    broadcast_in_dim x1, local copies, waits for them, and re-layouts, pair_device(): low_byte = jnp.maximum(positions - WIN, doc_starts - first_byte)[:, None]  1.02 us

profile of v2, /device:TPU:0, one launch (start us, length us, event | category | flops | bytes accessed | tf_op | source)
XLA Modules:
  0.0 50.3 jit_solution(11254758817696878582)
XLA Ops:
  0.0 0.7 %subtract_maximum_fusion = s32[1024]{0:T(1024)S(1)} fusion(s32[1024]{0:T(1024)} %param.20, s32[]{:T(128)S(6)} %mul.6), kind=kLoop, calls=%fused_computation.2 | loop fusion | flops 3072 | bytes 8196 | tf_op jit(solution)/shard_map/max | solution.py:377
  0.7 1.3 %broadcast_in_dim.17.gain = bf16[1,1024]{1,0:T(2,128)(2,1)} reshape(bf16[1024]{0:T(1024)(128)(2,1)} %param.21) | data formatting | bytes 4096 | tf_op jit(solution)/shard_map/broadcast_in_dim | solution.py:385
  2.0 1.3 %broadcast_in_dim.16.latent_gain = bf16[1,2048]{1,0:T(2,128)(2,1)} reshape(bf16[2048]{0:T(1024)(128)(2,1)} %param.16) | data formatting | bytes 8192 | tf_op jit(solution)/shard_map/broadcast_in_dim | solution.py:385
  3.3 0.7 %broadcast_subtract_fusion = s32[4096]{0:T(1024)S(1)} fusion(s32[4096]{0:T(1024)} %param.18, s32[]{:T(128)S(6)} %mul.6), kind=kLoop, calls=%fused_computation.1 | loop fusion | flops 4096 | bytes 32772 | tf_op jit(solution)/shard_map/sub | solution.py:379
  4.0 0.6 %fusion = s32[512]{0:T(512)} fusion(s32[]{:T(128)S(6)} %select_n.7, s32[4096]{0:T(1024)S(1)} %broadcast_subtract_fusion), kind=kLoop, calls=%fused_computation.3 | loop fusion | flops 1024 | bytes 18436 | tf_op jit(solution)/shard_map/jit(_where)/select_n | solution.py:382
  4.6 1.0 %copy.16.low_key = s32[1024,1]{1,0:T(8,128)} copy(s32[1024,1]{0,1:T(1,128)S(1)} %bitcast.2) | data formatting | bytes 8192 | tf_op jit(solution)/shard_map/broadcast_in_dim | solution.py:377
  5.6 42.4 %shard_map.145 = bf16[1024,512]{1,0:T(8,128)(2,1)} custom-call(bf16[256,2048]{1,0:T(8,128)(2,1)} %latent_h.1, bf16[2048,1024]{1,0:T(8,128)(2,1)} %proj_h.1, bf16[1024,1024]{1,0:T(8,128)(2,1)} %stream_h.1, bf16[1024,512]{1,0:T(8,128)(2,1)} %wk_h.1, bf16[1024,512]{1,0:T(8,128)(2,1)} %wv_h.1, bf16[1024,512]{1,0:T(8,128)(2,1)} %wq_h.1, bf16[1024,512]{1,0:T(8,128)(2,1)} %wc_h.1, ...), custom_call_target="tpu_custom_call" | custom-call | tf_op jit(solution)/shard_map/pallas_call | solution.py:387
  48.0 2.3 %copy.18 = bf16[1024,512]{1,0:T(8,128)(2,1)} copy(bf16[1024,512]{1,0:T(8,128)(2,1)} %shard_map.145) | data formatting | bytes 2097152

commit v3 on v2

--- a/solution.py
+++ b/solution.py
@@ -27,22 +27,37 @@
     return jnp.dot(left, right, preferred_element_type=F32)
 
 
-def pair_attend(query, keys, values, bias):
-    rows = query.shape[0]
-    low = lax.broadcasted_iota(jnp.int32, (rows, LANES), 1) < HD
+def score_pair(query, keys):
+    low = lax.broadcasted_iota(jnp.int32, query.shape, 1) < HD
     zero = jnp.zeros_like(query)
     scaled = query * jnp.asarray(HD**-0.5, BF16)
     both = jnp.concatenate([jnp.where(low, scaled, zero), jnp.where(low, zero, scaled)], axis=0)
-    scores = lax.dot_general(both, keys, (((1,), (1,)), ((), ())), preferred_element_type=F32)
+    return lax.dot_general(both, keys, (((1,), (1,)), ((), ())), preferred_element_type=F32)
+
+
+def mix_pair(scores, values, bias):
+    rows = bias.shape[0]
     wide = jnp.concatenate([values, jnp.ones_like(values)], axis=1)
-    mixed = []
-    for half in range(2):
-        one = scores[half * rows : (half + 1) * rows] + bias
+    totals = []
+    for part in range(2):
+        one = scores[part * rows : (part + 1) * rows] + bias
         top = jnp.max(one, axis=1, keepdims=True)
-        weights = jnp.exp(one - top).astype(BF16)
-        total = mm(weights, wide)
-        mixed.append(total[:, :LANES] / total[:, LANES:])
-    return jnp.where(low, mixed[0], mixed[1]).astype(BF16)
+        totals.append(mm(jnp.exp(one - top).astype(BF16), wide))
+    low = lax.broadcasted_iota(jnp.int32, (rows, LANES), 1) < HD
+    upper = jnp.where(low, totals[0][:, :LANES], totals[1][:, :LANES])
+    lower = jnp.where(low, totals[0][:, LANES:], totals[1][:, LANES:])
+    return (upper / lower).astype(BF16)
+
+
+def attend_pairs(query, rows, keys, values, near, bias, out, out_rows):
+    places = [slice(col, col + LANES) for col in range(0, query.shape[1], LANES)]
+    scores = score_pair(query[rows, places[0]], keys[near, places[0]])
+    for number, at in enumerate(places):
+        ready = scores
+        if number + 1 < len(places):
+            ahead = places[number + 1]
+            scores = score_pair(query[rows, ahead], keys[near, ahead])
+        out[out_rows, at] = mix_pair(ready, values[near, at], bias)
 
 
 def from_behind(array, axis, by):
@@ -158,10 +173,10 @@
 
 def layer_kernel(
     latent_h, proj_h, stream_h, wk_h, wv_h, wq_h, wc_h, ck_h, cv_h, so_h, co_h,
-    latent_gain, gain, starts, low_key, out,
+    latent_gain, gain, patch_starts, doc_starts, out,
     latent, proj, stream, wk, wv, wq, wc, ck, cv, so, co,
     halo, keys, values, queries, cross_rows, mixed, cross, sq_mine, sq_peer, part_mine, part_peer,
-    joined, patch_keys, patch_values, own, far, far_peer, local_sem, send_sem, recv_sem,
+    joined, patch_keys, patch_values, own, far, far_peer, starts, low_key, local_sem, send_sem, recv_sem,
 ):
     seg, width = stream.shape
     cols = wk.shape[1]
@@ -179,7 +194,7 @@
         (proj_h, proj), (ck_h, ck), (cv_h, cv), (so_h, so), (co_h, co),
     )
     loads = [pltpu.make_async_copy(a, b, local_sem.at[i]) for i, (a, b) in enumerate(pairs)]
-    for load in loads:
+    for load in loads[:6]:
         load.start()
 
     barrier = pltpu.get_barrier_semaphore()
@@ -220,6 +235,28 @@
     def _():
         halo_send.start()
 
+    first_byte = place_seq * seg
+    byte = lax.broadcasted_iota(jnp.int32, (LANES, LANES), 1)
+    for at in range(0, seg, LANES):
+        lowest = jnp.maximum(byte + (at - WIN), doc_starts[:, at : at + LANES] - first_byte)
+        low_key[at : at + LANES, :] = lowest.T
+    behind = pl.ds(pl.multiple_of(jnp.maximum(place_seq - 1, 0) * patch_dev, LANES), patch_dev)
+    own_patches = pl.ds(pl.multiple_of(place_seq * patch_dev, LANES), patch_dev)
+    ahead = pl.ds(pl.multiple_of(jnp.minimum(place_seq + 1, last) * patch_dev, LANES), LANES)
+    tight = jnp.concatenate(
+        [
+            jnp.where(has_left, patch_starts[:, behind] - first_byte, seg),
+            patch_starts[:, own_patches] - first_byte,
+            jnp.where(has_right, patch_starts[:, ahead] - first_byte, seg),
+        ],
+        axis=1,
+    )
+    span = tight.shape[1]
+    skipped = patch_dev - before
+    tight = pltpu.roll(jnp.broadcast_to(tight, (8, span)), span - skipped, 1)[:, : starts.shape[1]]
+    slot = lax.broadcasted_iota(jnp.int32, tight.shape, 1)
+    starts[...] = jnp.where(slot < joined.shape[0], tight, seg)
+
     loads[0].wait()
     widened = latent[...].astype(F32)
     square = jnp.sum(widened * widened, axis=1, keepdims=True)
@@ -228,11 +265,13 @@
 
     for load in loads[1:6]:
         load.wait()
+    for load in loads[6:]:
+        load.start()
 
     def project_rows(step, carry):
         rows = pl.ds(pl.multiple_of(step * QB, QB), QB)
         shifted = pl.ds(pl.multiple_of(step * QB + WIN, QB), QB)
-        hidden = norm_rows(stream[rows, :], gain[...])
+        hidden = norm_rows(stream[rows, :], gain[...][None, :])
         keys[shifted, :] = mm(hidden, wk[...]).astype(BF16)
         values[shifted, :] = mm(hidden, wv[...]).astype(BF16)
         queries[rows, :] = mm(hidden, wq[...]).astype(BF16)
@@ -244,7 +283,7 @@
     loads[6].wait()
     sq_swap.wait()
     scale = lax.rsqrt((sq_mine[:, :1] + sq_peer[:, :1]) / (2 * latent.shape[1]) + 1e-05)
-    normed = (latent[...].astype(F32) * scale * latent_gain[...].astype(F32)).astype(BF16)
+    normed = (latent[...].astype(F32) * scale * latent_gain[...][None, :].astype(F32)).astype(BF16)
     part_mine[...] = mm(normed, proj[...])
     part_swap.start()
 
@@ -255,11 +294,9 @@
     def self_rows(step, carry):
         base = pl.multiple_of(step * QB, QB)
         rows, near = pl.ds(base, QB), pl.ds(base, count)
-        allowed = (index <= row + WIN) & (index >= low_key[rows, :] + (WIN - base))
+        allowed = (index <= row + WIN) & (index >= low_key[rows, :1] + (WIN - base))
         bias = jnp.where(allowed, 0.0, FAR).astype(F32)
-        for col in range(0, cols, LANES):
-            at = slice(col, col + LANES)
-            mixed[rows, at] = pair_attend(queries[rows, at], keys[near, at], values[near, at], bias)
+        attend_pairs(queries, rows, keys, values, near, bias, mixed, rows)
         return carry
 
     inner = WIN // QB
@@ -303,7 +340,7 @@
     def _():
         joined[back, :] = jnp.zeros((after, width), BF16)
 
-    hidden = norm_rows(halo[...], gain[...])
+    hidden = norm_rows(halo[...], gain[...][None, :])
     keys[:WIN, :] = mm(hidden, wk[...]).astype(BF16)
     values[:WIN, :] = mm(hidden, wv[...]).astype(BF16)
     lax.fori_loop(0, inner, self_rows, 0)
@@ -339,14 +376,10 @@
         rows = pl.ds(pl.multiple_of(step * QB, QB), QB)
         base = pl.multiple_of(lax.rem(lax.div(step, inner), 2) * LANES, LANES)
         near = pl.ds(base, slots)
-        first = starts[:, near]
-        allowed = (first <= slot_row + step * QB) & (first >= low_key[rows, :])
+        first = starts[:1, near]
+        allowed = (first <= slot_row + step * QB) & (first >= low_key[rows, :1])
         bias = jnp.where(allowed, 0.0, FAR).astype(F32)
-        for col in range(0, cols, LANES):
-            at = slice(col, col + LANES)
-            cross[:, at] = pair_attend(
-                cross_rows[rows, at], patch_keys[near, at], patch_values[near, at], bias
-            )
+        attend_pairs(cross_rows, rows, patch_keys, patch_values, near, bias, cross, slice(None))
         far[rows, :] = (mm(mixed[rows, :], so[:, there]) + mm(cross[...], co[:, there])).astype(BF16)
         out_swap(step).start()
         own[rows, :] = mm(mixed[rows, :], so[:, here]) + mm(cross[...], co[:, here])
@@ -359,6 +392,12 @@
 
     lax.fori_loop(0, seg // QB, cross_block, 0)
     finish(seg // QB - 1)
+
+
+def write_kernel(source, target, sem):
+    copy = pltpu.make_async_copy(source, target, sem)
+    copy.start()
+    copy.wait()
 
 
 def pair_device(
@@ -368,23 +407,14 @@
     seg, width = stream.shape
     patch_dev, features = latent.shape
     cols = self_query.shape[1]
-    first_byte = lax.axis_index("seq") * seg
     before, after = WIN * patch_dev // seg + DRIFT, DRIFT
     used = before + patch_dev + after
     slots = (used + LANES - 1) // LANES * LANES
 
-    positions = jnp.arange(seg, dtype=jnp.int32)
-    low_byte = jnp.maximum(positions - WIN, doc_starts - first_byte)[:, None]
-    padded = jnp.pad(
-        patch_starts - first_byte, (before, slots), constant_values=seg * (lax.axis_size("seq") + 1)
-    )
-    window = lax.dynamic_slice_in_dim(padded, lax.axis_index("seq") * patch_dev, slots, 0)
-    window = jnp.where(jnp.arange(slots) < used, window, seg)[None, :]
-
     big = (latent, proj_weight, stream, self_key, self_value, self_query, cross_query, cross_key, cross_value, self_out, cross_out)
-    small = (latent_gain[None, :], stream_gain[None, :], window, low_byte)
+    small = (latent_gain, stream_gain, patch_starts[None, :], doc_starts[None, :])
     blocks = seg // QB
-    return pl.pallas_call(
+    update = pl.pallas_call(
         layer_kernel,
         in_specs=[pl.BlockSpec(memory_space=pl.ANY)] * len(big)
         + [pl.BlockSpec(memory_space=pltpu.VMEM)] * len(small),
@@ -409,6 +439,8 @@
             pltpu.VMEM((seg, cols), F32),
             pltpu.VMEM((seg, cols), BF16),
             pltpu.VMEM((seg, cols), BF16),
+            pltpu.VMEM((8, slots), jnp.int32),
+            pltpu.VMEM((seg, LANES), jnp.int32),
             pltpu.SemaphoreType.DMA((len(big),)),
             pltpu.SemaphoreType.DMA((8 + blocks,)),
             pltpu.SemaphoreType.DMA((8 + blocks,)),
@@ -417,6 +449,13 @@
             collective_id=0, has_side_effects=True, vmem_limit_bytes=60 << 20
         ),
     )(*big, *small)
+    return pl.pallas_call(
+        write_kernel,
+        in_specs=[pl.BlockSpec(memory_space=pltpu.VMEM)],
+        out_specs=pl.BlockSpec(memory_space=pl.ANY),
+        out_shape=jax.ShapeDtypeStruct((seg, cols), BF16),
+        scratch_shapes=[pltpu.SemaphoreType.DMA],
+    )(update)
 
 
 def solution(mesh):

time: 50.7 us -> 42.4 us (0.84)
  local copies, waits for them, and re-layouts: 5.85 us -> 0 us
  other arithmetic: 2.05 us -> 0 us
    broadcast_in_dim x3 -> x0, local copies, waits for them, and re-layouts: 3.58 us -> none  [the longest x2 2.56 us: pair_device(): small = (latent_gain[None, :], stream_gain[None, :], window, low_byte)]
    pallas_call x1, Pallas kernels: 42.4 us -> 39.9 us  [pair_device(): pl.pallas_call(layer_kernel, in_specs=[pl.BlockSpec(memory_space=pl.ANY)]...]
    unnamed x1 -> x0, local copies, waits for them, and re-layouts: 2.26 us -> none
    pallas_call x0 -> x1, Pallas kernels: none -> 2.2 us  [pair_device(): pl.pallas_call(write_kernel, in_specs=[pl.BlockSpec(memory_space=pltpu.VM...]
    sub x1 -> x0, other arithmetic: 0.72 us -> none  [pair_device(): patch_starts - first_byte]
    max x1 -> x0, other arithmetic: 0.69 us -> none  [pair_device(): low_byte = jnp.maximum(positions - WIN, doc_starts - first_byte)[:, None]]
    select_n x1 -> x0, other arithmetic: 0.64 us -> none  [pair_device(): window = jnp.where(jnp.arange(slots) < used, window, seg)[None, :]]
where the time goes in v3:
time: 42.4 us; the launch traced here: 42.2 us
  Pallas kernels  42.1 us (99%)
    pallas_call x1, Pallas kernels, pair_device(): pl.pallas_call(layer_kernel, in_specs=[pl.BlockSpec(memory_space=pl.ANY)]...  39.9 us
    pallas_call x1, Pallas kernels, pair_device(): pl.pallas_call(write_kernel, in_specs=[pl.BlockSpec(memory_space=pltpu.VM...  2.2 us

profile of v3, /device:TPU:0, one launch (start us, length us, event | category | flops | bytes accessed | tf_op | source)
XLA Modules:
  0.0 42.2 jit_solution(14129005166094577938)
XLA Ops:
  0.0 39.9 %shard_map.145.source = bf16[1024,512]{1,0:T(8,128)(2,1)} custom-call(bf16[256,2048]{1,0:T(8,128)(2,1)} %latent_h.1, bf16[2048,1024]{1,0:T(8,128)(2,1)} %proj_h.1, bf16[1024,1024]{1,0:T(8,128)(2,1)} %stream_h.1, bf16[1024,512]{1,0:T(8,128)(2,1)} %wk_h.1, bf16[1024,512]{1,0:T(8,128)(2,1)} %wv_h.1, bf16[1024,512]{1,0:T(8,128)(2,1)} %wq_h.1, ...), custom_call_target="tpu_custom_call" | custom-call | tf_op jit(solution)/shard_map/pallas_call | solution.py:417
  39.9 2.2 %shard_map.146 = bf16[1024,512]{1,0:T(8,128)(2,1)} custom-call(bf16[1024,512]{1,0:T(8,128)(2,1)} %shard_map.145.source), custom_call_target="tpu_custom_call" | custom-call | tf_op jit(solution)/shard_map/pallas_call | solution.py:452

commit v4 on v3

--- a/solution.py
+++ b/solution.py
@@ -176,7 +176,7 @@
     latent_gain, gain, patch_starts, doc_starts, out,
     latent, proj, stream, wk, wv, wq, wc, ck, cv, so, co,
     halo, keys, values, queries, cross_rows, mixed, cross, sq_mine, sq_peer, part_mine, part_peer,
-    joined, patch_keys, patch_values, own, far, far_peer, starts, low_key, local_sem, send_sem, recv_sem,
+    joined, patch_keys, patch_values, own, far, far_peer, starts, low_key, done, done_sem, local_sem, send_sem, recv_sem,
 ):
     seg, width = stream.shape
     cols = wk.shape[1]
@@ -367,10 +367,15 @@
         rows = pl.ds(pl.multiple_of(step * QB, QB), QB)
         return send(far.at[rows, :], far_peer.at[rows, :], 8 + step, peer)
 
+    def write_out(step):
+        rows = pl.ds(pl.multiple_of(step * QB, QB), QB)
+        return pltpu.make_async_copy(done.at[rows, :], out.at[rows, :], done_sem.at[step])
+
     def finish(step):
         out_swap(step).wait()
         rows = pl.ds(pl.multiple_of(step * QB, QB), QB)
-        out[rows, :] = (own[rows, :] + far_peer[rows, :].astype(F32)).astype(BF16)
+        done[rows, :] = (own[rows, :] + far_peer[rows, :].astype(F32)).astype(BF16)
+        write_out(step).start()
 
     def cross_block(step, carry):
         rows = pl.ds(pl.multiple_of(step * QB, QB), QB)
@@ -392,12 +397,23 @@
 
     lax.fori_loop(0, seg // QB, cross_block, 0)
     finish(seg // QB - 1)
-
-
-def write_kernel(source, target, sem):
-    copy = pltpu.make_async_copy(source, target, sem)
-    copy.start()
-    copy.wait()
+    for step in range(seg // QB):
+        write_out(step).wait()
+
+
+def write_kernel(source, target, held, in_sem, out_sem):
+    blocks = in_sem.shape[0]
+    size = source.shape[0] // blocks
+    rows = [pl.ds(block * size, size) for block in range(blocks)]
+    takes = [pltpu.make_async_copy(source.at[r, :], held.at[r, :], in_sem.at[i]) for i, r in enumerate(rows)]
+    gives = [pltpu.make_async_copy(held.at[r, :], target.at[r, :], out_sem.at[i]) for i, r in enumerate(rows)]
+    for take in takes:
+        take.start()
+    for take, give in zip(takes, gives):
+        take.wait()
+        give.start()
+    for give in gives:
+        give.wait()
 
 
 def pair_device(
@@ -418,7 +434,7 @@
         layer_kernel,
         in_specs=[pl.BlockSpec(memory_space=pl.ANY)] * len(big)
         + [pl.BlockSpec(memory_space=pltpu.VMEM)] * len(small),
-        out_specs=pl.BlockSpec(memory_space=pltpu.VMEM),
+        out_specs=pl.BlockSpec(memory_space=pl.ANY),
         out_shape=jax.ShapeDtypeStruct((seg, cols), BF16),
         scratch_shapes=[pltpu.VMEM(array.shape, BF16) for array in big]
         + [
@@ -441,6 +457,8 @@
             pltpu.VMEM((seg, cols), BF16),
             pltpu.VMEM((8, slots), jnp.int32),
             pltpu.VMEM((seg, LANES), jnp.int32),
+            pltpu.VMEM((seg, cols), BF16),
+            pltpu.SemaphoreType.DMA((blocks,)),
             pltpu.SemaphoreType.DMA((len(big),)),
             pltpu.SemaphoreType.DMA((8 + blocks,)),
             pltpu.SemaphoreType.DMA((8 + blocks,)),
@@ -451,10 +469,14 @@
     )(*big, *small)
     return pl.pallas_call(
         write_kernel,
-        in_specs=[pl.BlockSpec(memory_space=pltpu.VMEM)],
+        in_specs=[pl.BlockSpec(memory_space=pl.ANY)],
         out_specs=pl.BlockSpec(memory_space=pl.ANY),
         out_shape=jax.ShapeDtypeStruct((seg, cols), BF16),
-        scratch_shapes=[pltpu.SemaphoreType.DMA],
+        scratch_shapes=[
+            pltpu.VMEM((seg, cols), BF16),
+            pltpu.SemaphoreType.DMA((2 * blocks,)),
+            pltpu.SemaphoreType.DMA((2 * blocks,)),
+        ],
     )(update)
 
 

time: 42.4 us -> 42.1 us (level)
  no operation moved by 1% of the time
where the time goes in v4:
time: 42.1 us; the launch traced here: 41.9 us
  Pallas kernels  41.7 us (99%)
    pallas_call x1, Pallas kernels, pair_device(): pl.pallas_call(layer_kernel, in_specs=[pl.BlockSpec(memory_space=pl.ANY)]...  39.6 us
    pallas_call x1, Pallas kernels, pair_device(): pl.pallas_call(write_kernel, in_specs=[pl.BlockSpec(memory_space=pl.ANY)]...  2.09 us

profile of v4, /device:TPU:0, one launch (start us, length us, event | category | flops | bytes accessed | tf_op | source)
XLA Modules:
  0.0 41.9 jit_solution(16409588061479561229)
XLA Ops:
  0.0 39.6 %shard_map.145.source = bf16[1024,512]{1,0:T(8,128)(2,1)} custom-call(bf16[256,2048]{1,0:T(8,128)(2,1)} %latent_h.1, bf16[2048,1024]{1,0:T(8,128)(2,1)} %proj_h.1, bf16[1024,1024]{1,0:T(8,128)(2,1)} %stream_h.1, bf16[1024,512]{1,0:T(8,128)(2,1)} %wk_h.1, bf16[1024,512]{1,0:T(8,128)(2,1)} %wv_h.1, bf16[1024,512]{1,0:T(8,128)(2,1)} %wq_h.1, ...), custom_call_target="tpu_custom_call" | custom-call | tf_op jit(solution)/shard_map/pallas_call | solution.py:433
  39.6 2.1 %shard_map.146 = bf16[1024,512]{1,0:T(8,128)(2,1)} custom-call(bf16[1024,512]{1,0:T(8,128)(2,1)} %shard_map.145.source), custom_call_target="tpu_custom_call" | custom-call | tf_op jit(solution)/shard_map/pallas_call | solution.py:470
